TPU v7x, 512 devices: a whole 4x8x8 slice. The times are simulated.
512 devices in a mesh: seq: 32 (over z_lo, y), tp: 16 (over x, z_hi, core).
Axes of the slice: x: 4, y: 8, z: 8 (z_hi: 2, z_lo: 4; z = z_hi * 4 + z_lo), core: 2. Of those that a mesh axis runs over, the one named last changes fastest.
Arguments:
- latents: bfloat16 [4096, 3072], P('seq', 'tp'), may hold values from -6 to 6
- lengths: int32 [2], replicated, may hold values from 1 to 3072, 4096 in all
- t_index: int32 [2], replicated, may hold values from 0 to 6
- mod_scale: float32 [3072], replicated, may hold values from -2 to 2
- q_weight: bfloat16 [3072, 2048], P(None, 'tp'), may hold values from -0.109375 to 0.109375
- k_weight: bfloat16 [3072, 2048], P(None, 'tp'), may hold values from -0.109375 to 0.109375
- v_weight: bfloat16 [3072, 2048], P(None, 'tp'), may hold values from -0.109375 to 0.109375
- out_weight: bfloat16 [2048, 3072], P('tp'), may hold values from -0.1875 to 0.1875
- q_gain: float32 [128], replicated, may hold values from 0.6 to 2.4
- k_gain: float32 [128], replicated, may hold values from 0.6 to 2.4
- student_weight: bfloat16 [3072, 3072], P('tp'), may hold values from -0.15625 to 0.15625
Outputs:
- target: bfloat16 [4096, 3072], P('seq', 'tp')
- student_velocity: bfloat16 [4096, 3072], P('seq', 'tp')
- loss: float32 [], replicated
Inputs may be any that keep to these rules, and one draw needn't show every extreme that they name: lengths sum to 4096.
All inputs are finite; a program needn't handle non-finite values.
Results may differ from a plain program's by a relative error of at most 0.024.
Values may be sent and summed in bfloat16 or wider, within the bound.
A program may use at most 64 MiB of HBM per device.

v0:
```python
import functools
import math

import jax
import jax.numpy as jnp
from jax import lax
from jax.sharding import Mesh
from jax.sharding import PartitionSpec as P

TGRID = 8
SEQ = ("seq_0", "seq_1")
TP = ("tp_0", "tp_1", "tp_2")
SEQ_TP = ("seq_0", "seq_1", "tp_0", "tp_1", "tp_2")


epsilon = 1e-06
kinetic_weight = 0.1


def in_one_piece(arrays, axis, dim, along):
    widths = [a.shape[along] for a in arrays]
    both = jnp.concatenate(arrays, axis=along)
    whole = lax.all_gather(both, axis, axis=dim, tiled=True)
    return tuple(jnp.split(whole, [sum(widths[:k]) for k in range(1, len(widths))], axis=along))


def from_everyone(value, axis):
    length = lax.axis_size(axis)
    return lax.all_to_all(
        jnp.broadcast_to(value[None], (length, *value.shape)), axis, 0, 0, tiled=True
    )


def laid_out(pieces, dim):
    pieces = jnp.moveaxis(pieces, 0, dim)
    lengths = pieces.shape
    return pieces.reshape(*lengths[:dim], lengths[dim] * lengths[dim + 1], *lengths[dim + 2 :])


def gathered_copies(value, axis, dim):
    pieces = from_everyone(value, axis)
    return laid_out(pieces, dim)


def over_axes(value, axes):
    return functools.reduce(lax.psum, axes, value)


def image_index(positions, image_ends):
    return jnp.sum((positions[:, None] >= image_ends[None, :]).astype(jnp.int32), axis=1)


def head_norm(projected, gain):
    shaped = projected.reshape(projected.shape[0], -1, gain.shape[0])
    normed = shaped * lax.rsqrt(jnp.mean(shaped * shaped, axis=-1, keepdims=True) + epsilon) * gain
    return normed.astype(jnp.bfloat16)


def grouped_columns(whole_left, right_columns, groups):
    row_count = whole_left.shape[0]
    group_width = whole_left.shape[1] // groups
    left_groups = whole_left.reshape(row_count, groups, group_width)
    right_groups = right_columns.reshape(groups, group_width, right_columns.shape[1])
    terms = jnp.einsum(
        "tng,ngd->tnd", left_groups, right_groups, preferred_element_type=jnp.float32
    ).astype(jnp.bfloat16)
    terms = lax.optimization_barrier(terms)
    return jnp.sum(terms.astype(jnp.float32), axis=1)


def teacher(
    state, times, query_image, image_ends, mod_scale, q_weight, k_weight, v_weight, q_gain, k_gain
):
    row_count = state.shape[0]
    head_dim = q_gain.shape[0]
    state32 = state.astype(jnp.float32)
    normed = state32 * lax.rsqrt(jnp.mean(state32 * state32, axis=1, keepdims=True) + epsilon)
    hidden = (normed * (1.0 + times[:, None] * mod_scale[None, :])).astype(jnp.bfloat16)
    queries = head_norm(jnp.dot(hidden, q_weight, preferred_element_type=jnp.float32), q_gain)
    key_rows = head_norm(jnp.dot(hidden, k_weight, preferred_element_type=jnp.float32), k_gain)
    key_rows = key_rows.reshape(row_count, -1)
    value_rows = jnp.dot(hidden, v_weight, preferred_element_type=jnp.float32).astype(jnp.bfloat16)
    heads_here = queries.shape[1]
    score_scale = 1.0 / math.sqrt(head_dim)
    key_block, value_block = in_one_piece((key_rows, value_rows), SEQ, 0, 1)
    running_max = jnp.full((row_count, heads_here), -1e30, jnp.float32)
    count = key_block.shape[0]
    key_image = image_index(jnp.arange(count, dtype=jnp.int32), image_ends)
    key_heads = key_block.reshape(count, heads_here, head_dim)
    value_heads = value_block.reshape(count, heads_here, head_dim)
    same_image = (query_image[:, None] == key_image[None, :])[:, None, :]
    scores = (
        jnp.einsum("qhd,khd->qhk", queries, key_heads, preferred_element_type=jnp.float32)
        * score_scale
    )
    scores = jnp.where(same_image, scores, -1e30)
    new_max = jnp.maximum(running_max, jnp.max(scores, axis=2))
    weights = jnp.where(same_image, jnp.exp(scores - new_max[:, :, None]), 0.0)
    new_total = jnp.sum(weights, axis=2)
    product = jnp.einsum(
        "qhk,khd->qhd",
        weights.astype(jnp.bfloat16),
        value_heads,
        preferred_element_type=jnp.float32,
    )
    mixed = (product / new_total[:, :, None]).astype(jnp.bfloat16).reshape(row_count, -1)
    return (mixed, hidden)


def on_device(
    latents,
    lengths,
    t_index,
    mod_scale,
    q_weight,
    k_weight,
    v_weight,
    out_weight,
    q_gain,
    k_gain,
    student_weight,
):
    row_count, width_here = latents.shape
    tp_count = lax.axis_size(TP)
    image_ends = jnp.cumsum(lengths)
    row_offset = lax.axis_index(SEQ) * row_count
    query_image = image_index(row_offset + jnp.arange(row_count, dtype=jnp.int32), image_ends)
    one_hot = (
        query_image[:, None] == jnp.arange(lengths.shape[0], dtype=jnp.int32)[None, :]
    ).astype(jnp.float32)
    start_times = jnp.sum(one_hot * (t_index.astype(jnp.float32) / TGRID)[None, :], axis=1)
    step_size = 1.0 / TGRID
    whole_rows = lax.all_gather(latents, TP, axis=1, tiled=True)
    velocities = []
    first_hidden = whole_rows
    out_columns, student_columns = (
        lax.all_to_all(out_weight, TP, split_axis=1, concat_axis=0, tiled=True),
        lax.all_to_all(student_weight, TP, split_axis=1, concat_axis=0, tiled=True),
    )
    state_shard = latents
    for euler_index in range(2):
        if euler_index == 1:
            whole_rows = lax.all_gather(state_shard, TP, axis=1, tiled=True)
        mixed, hidden = teacher(
            whole_rows,
            start_times + euler_index * step_size,
            query_image,
            image_ends,
            mod_scale,
            q_weight,
            k_weight,
            v_weight,
            q_gain,
            k_gain,
        )
        if euler_index == 0:
            first_hidden = hidden
        all_heads = gathered_copies(mixed, TP, 1)
        velocity = grouped_columns(all_heads, out_columns, tp_count).astype(jnp.bfloat16)
        velocities.append(velocity)
        state_shard = (
            latents.astype(jnp.float32) + step_size * velocity.astype(jnp.float32)
        ).astype(jnp.bfloat16)
    student_velocity = grouped_columns(first_hidden, student_columns, tp_count).astype(jnp.bfloat16)
    target = (0.5 * (velocities[0].astype(jnp.float32) + velocities[1].astype(jnp.float32))).astype(
        jnp.bfloat16
    )
    student32 = student_velocity.astype(jnp.float32)
    residual = student32 - target.astype(jnp.float32)
    per_token = jnp.sum(residual * residual, axis=1) + kinetic_weight * jnp.sum(
        student32 * student32, axis=1
    )
    image_part = jnp.sum(one_hot * per_token[:, None], axis=0)
    image_sum = over_axes(image_part, SEQ_TP)
    loss = jnp.mean(image_sum / (lengths.astype(jnp.float32) * mod_scale.shape[0]))
    return (target, student_velocity, loss)


def solution(mesh):
    torus = Mesh(mesh.devices.reshape(4, 8, 4, 2, 2), ("seq_0", "seq_1", "tp_0", "tp_1", "tp_2"))
    in_specs = (
        P(SEQ, TP),
        P(),
        P(),
        P(),
        P(None, TP),
        P(None, TP),
        P(None, TP),
        P(TP, None),
        P(),
        P(),
        P(TP, None),
    )
    out_specs = (P(SEQ, TP), P(SEQ, TP), P())
    return jax.shard_map(
        on_device, mesh=torus, in_specs=in_specs, out_specs=out_specs, check_vma=False
    )
```

profile of v0, /device:TPU:1, one launch (start us, length us, event | category | flops | bytes accessed | tf_op | source)
XLA Modules:
  0.0 472.0 jit_solution(12956411148066289239)
XLA Ops:
  7.2 46.2 %all_gather.12 = bf16[128,3072]{0,1:T(8,128)(2,1)S(1)} all-gather(bf16[128,192]{0,1:T(8,128)(2,1)} %param.11), channel_id=1, replica_groups=mesh['seq_0'=4,'seq_1'=8,'tp_0'=4,'tp_1'=2,'tp_2'=2] {'tp_0','tp_1','tp_2'}, dimensions={1}, use_global_device_ids=true | all-gather | bytes 835584 | tf_op jit(solution)/shard_map/all_gather | solution.py:133
  59.6 3.6 all-to-all-start.1
  63.2 1.6 multiply_reduce_fusion.2
  64.9 99.5 %all-gather.3.cloned.1.call-done = bf16[4096,256]{0,1:T(8,128)(2,1)} async-done(((bf16[128,256]{0,1:T(8,128)(2,1)}), bf16[4096,256]{0,1:T(8,128)(2,1)}) %all-gather.3.cloned.1.call-update) | async-done | bytes 2097168 | tf_op jit(solution)/shard_map/all_gather | solution.py:23
  164.3 2.3 fusion.72
  166.6 1.9 fusion.4
  170.5 25.1 %all-to-all-start = ((bf16[16,128,128]{2,1,0:T(8,128)(2,1)}), bf16[16,128,128]{2,1,0:T(8,128)(2,1)}, u32[]{:S(2)}, u32[]{:S(2)}) async-start(bf16[16,128,128]{2,1,0:T(8,128)(2,1)} %broadcast_in_dim.20), calls=%async_computation | async-start | bytes 1048576 | tf_op jit(solution)/shard_map/all_to_all | solution.py:29
  195.7 16.0 %all-to-all-done = bf16[16,128,128]{2,1,0:T(8,128)(2,1)} async-done(((bf16[16,128,128]{2,1,0:T(8,128)(2,1)}), bf16[16,128,128]{2,1,0:T(8,128)(2,1)}, u32[]{:S(2)}, u32[]{:S(2)}) %all-to-all-start) | async-done | bytes 524320 | tf_op jit(solution)/shard_map/all_to_all | solution.py:29
  213.3 33.6 %all_gather.14 = bf16[128,3072]{0,1:T(8,128)(2,1)S(1)} all-gather(bf16[128,192]{0,1:T(8,128)(2,1)S(1)} %fusion.51), channel_id=1, replica_groups=mesh['seq_0'=4,'seq_1'=8,'tp_0'=4,'tp_1'=2,'tp_2'=2] {'tp_0','tp_1','tp_2'}, dimensions={1}, use_global_device_ids=true | all-gather | bytes 835584 | tf_op jit(solution)/shard_map/all_gather | solution.py:143
  247.3 2.0 convolution_convert_fusion.2
  250.9 2.5 copy.21
  253.5 9.4 %all-to-all-start.3 = ((bf16[192,16,192]{0,2,1:T(8,128)(2,1)}), bf16[192,16,192]{0,2,1:T(8,128)(2,1)}, u32[]{:S(2)}, u32[]{:S(2)}) async-start(bf16[192,16,192]{0,2,1:T(8,128)(2,1)} %bitcast.82), calls=%async_computation.3 | async-start | bytes 3145728 | tf_op jit(solution)/shard_map/all_to_all | solution.py:138
  262.8 2.0 multiply_reduce_fusion
  264.8 98.7 %all-gather.5.cloned.1.call-done = bf16[4096,256]{0,1:T(8,128)(2,1)} async-done(((bf16[128,256]{0,1:T(8,128)(2,1)}), bf16[4096,256]{0,1:T(8,128)(2,1)}) %all-gather.5.cloned.1.call-update) | async-done | bytes 2097168 | tf_op jit(solution)/shard_map/all_gather | solution.py:23
  363.5 2.3 fusion.73
  365.8 1.9 fusion.6
  369.6 24.2 %all-to-all-start.2 = ((bf16[16,128,128]{2,1,0:T(8,128)(2,1)}), bf16[16,128,128]{2,1,0:T(8,128)(2,1)}, u32[]{:S(2)}, u32[]{:S(2)}) async-start(bf16[16,128,128]{2,1,0:T(8,128)(2,1)} %broadcast_in_dim.22), calls=%async_computation.2 | async-start | bytes 1048576 | tf_op jit(solution)/shard_map/all_to_all | solution.py:29
  393.8 2.0 fusion.21
  395.9 13.0 %all-to-all-done.2 = bf16[16,128,128]{2,1,0:T(8,128)(2,1)} async-done(((bf16[16,128,128]{2,1,0:T(8,128)(2,1)}), bf16[16,128,128]{2,1,0:T(8,128)(2,1)}, u32[]{:S(2)}, u32[]{:S(2)}) %all-to-all-start.2) | async-done | bytes 524320 | tf_op jit(solution)/shard_map/all_to_all | solution.py:29
  411.3 11.7 %psum.35 = f32[2]{0:T(128)S(1)} all-reduce(f32[2]{0:T(128)S(1)} %select_reduce_fusion), channel_id=1, replica_groups=mesh['seq_0'=4,'seq_1'=8,'tp_0'=4,'tp_1'=2,'tp_2'=2] {'seq_0'}, use_global_device_ids=true, to_apply=%region_20.21 | all-reduce | flops 2 | bytes 16 | tf_op jit(solution)/shard_map/psum | solution.py:46
  423.0 13.4 %psum.36 = f32[2]{0:T(128)S(1)} all-reduce(f32[2]{0:T(128)S(1)} %psum.35), channel_id=1, replica_groups=mesh['seq_0'=4,'seq_1'=8,'tp_0'=4,'tp_1'=2,'tp_2'=2] {'seq_1'}, use_global_device_ids=true, to_apply=%region_21.22 | all-reduce | flops 2 | bytes 16 | tf_op jit(solution)/shard_map/psum | solution.py:46
  436.4 6.6 %psum.37 = f32[2]{0:T(128)S(1)} all-reduce(f32[2]{0:T(128)S(1)} %psum.36), channel_id=1, replica_groups=mesh['seq_0'=4,'seq_1'=8,'tp_0'=4,'tp_1'=2,'tp_2'=2] {'tp_0'}, use_global_device_ids=true, to_apply=%region_22.23 | all-reduce | flops 2 | bytes 16 | tf_op jit(solution)/shard_map/psum | solution.py:46
  443.0 7.7 %psum.38 = f32[2]{0:T(128)S(1)} all-reduce(f32[2]{0:T(128)S(1)} %psum.37), channel_id=1, replica_groups=mesh['seq_0'=4,'seq_1'=8,'tp_0'=4,'tp_1'=2,'tp_2'=2] {'tp_1'}, use_global_device_ids=true, to_apply=%region_23.24 | all-reduce | flops 2 | bytes 16 | tf_op jit(solution)/shard_map/psum | solution.py:46
  450.7 12.1 %psum.39 = f32[2]{0:T(128)S(1)} all-reduce(f32[2]{0:T(128)S(1)} %psum.38), channel_id=1, replica_groups=mesh['seq_0'=4,'seq_1'=8,'tp_0'=4,'tp_1'=2,'tp_2'=2] {'tp_2'}, use_global_device_ids=true, to_apply=%region_24.25 | all-reduce | flops 2 | bytes 16 | tf_op jit(solution)/shard_map/psum | solution.py:46
  (70 shorter events, 16.9 us)
Async XLA Ops:
  7.2 50.1 %copy-start = (bf16[3072,128]{1,0:T(8,128)(2,1)S(1)}, bf16[3072,128]{1,0:T(8,128)(2,1)}, u32[]{:S(2)}) copy-start(bf16[3072,128]{1,0:T(8,128)(2,1)} %param.16) | copy-start | bytes 2359300
  7.2 49.6 %copy-start.2 = (bf16[3072,128]{1,0:T(8,128)(2,1)S(1)}, bf16[3072,128]{1,0:T(8,128)(2,1)}, u32[]{:S(2)}) copy-start(bf16[3072,128]{1,0:T(8,128)(2,1)} %param.17) | copy-start | bytes 2359300
  7.2 157.1 %all-gather.3.cloned.1.call-start = ((), (), s32[]{:S(2)}) async-start(), calls=%async_computation.4 | async-start | bytes 2162688 | tf_op jit(solution)/shard_map/all_gather | solution.py:23
  55.6 2.1 copy-start.6
  56.8 1.6 copy-start.1
  58.4 105.9 %copy-start.9 = (f32[128]{0:T(128)S(1)}, f32[128]{0:T(128)}, u32[]{:S(2)}) copy-start(f32[128]{0:T(128)} %param.19) | copy-start | bytes 1540
  59.6 109.9 %all-to-all-start.1 = ((bf16[128,16,192]{0,2,1:T(8,128)(2,1)}), bf16[128,16,192]{0,2,1:T(8,128)(2,1)S(1)}, u32[]{:S(2)}, u32[]{:S(2)}) async-start(bf16[128,16,192]{0,2,1:T(8,128)(2,1)} %bitcast.9), calls=%async_computation.1 | async-start | bytes 1572864 | tf_op jit(solution)/shard_map/all_to_all | solution.py:137
  164.3 4.2 copy-start.8
  170.5 42.8 %copy-start.3 = (bf16[128,192]{0,1:T(8,128)(2,1)S(1)}, bf16[128,192]{0,1:T(8,128)(2,1)}, u32[]{:S(2)}) copy-start(bf16[128,192]{0,1:T(8,128)(2,1)} %param.11) | copy-start | bytes 147460
  170.5 41.2 %all-to-all-start = ((bf16[16,128,128]{2,1,0:T(8,128)(2,1)}), bf16[16,128,128]{2,1,0:T(8,128)(2,1)}, u32[]{:S(2)}, u32[]{:S(2)}) async-start(bf16[16,128,128]{2,1,0:T(8,128)(2,1)} %broadcast_in_dim.20), calls=%async_computation | async-start | bytes 1048576 | tf_op jit(solution)/shard_map/all_to_all | solution.py:29
  195.6 167.9 %all-gather.5.cloned.1.call-start = ((), (), s32[]{:S(2)}) async-start(), calls=%async_computation.5 | async-start | bytes 2162688 | tf_op jit(solution)/shard_map/all_gather | solution.py:23
  195.6 51.7 %copy-start.5 = (f32[3072]{0:T(1024)S(1)}, f32[3072]{0:T(1024)}, u32[]{:S(2)}) copy-start(f32[3072]{0:T(1024)} %param.14) | copy-start | bytes 36868
  253.5 115.2 %all-to-all-start.3 = ((bf16[192,16,192]{0,2,1:T(8,128)(2,1)}), bf16[192,16,192]{0,2,1:T(8,128)(2,1)}, u32[]{:S(2)}, u32[]{:S(2)}) async-start(bf16[192,16,192]{0,2,1:T(8,128)(2,1)} %bitcast.82), calls=%async_computation.3 | async-start | bytes 3145728 | tf_op jit(solution)/shard_map/all_to_all | solution.py:138
  363.5 4.2 copy-start.7
  369.6 39.2 %all-to-all-start.2 = ((bf16[16,128,128]{2,1,0:T(8,128)(2,1)}), bf16[16,128,128]{2,1,0:T(8,128)(2,1)}, u32[]{:S(2)}, u32[]{:S(2)}) async-start(bf16[16,128,128]{2,1,0:T(8,128)(2,1)} %broadcast_in_dim.22), calls=%async_computation.2 | async-start | bytes 1048576 | tf_op jit(solution)/shard_map/all_to_all | solution.py:29
  395.8 67.0 %copy-start.10 = (s32[2]{0:T(128)S(1)}, s32[2]{0:T(128)}, u32[]{:S(2)}) copy-start(s32[2]{0:T(128)} %param.12) | copy-start | bytes 28
  395.9 68.1 %copy-start.4 = (bf16[128,192]{0,1:T(8,128)(2,1)}, bf16[128,192]{0,1:T(8,128)(2,1)S(1)}, u32[]{:S(2)}) copy-start(bf16[128,192]{0,1:T(8,128)(2,1)S(1)} %reduce_sum.188) | copy-start | bytes 147460
Sparse Core Ops, SparseCore 0:
  58.5 105.7 all-gather.2
  251.1 112.4 all-gather.4
where the time goes:
time: 473 us; the launch traced here: 472 us
  waiting for transfers between devices  227 us (48%)
  blocking collectives  131 us (28%)
  starting transfers between devices  62.3 us (13%)
  matrix products  18.5 us (4%)
  between operations  16.1 us (3%)
  other arithmetic  10.8 us (2%)
  local copies, waits for them, and re-layouts  5.83 us (1%)
    all_gather x2, waiting for transfers between devices, in_one_piece(): whole = lax.all_gather(both, axis, axis=dim, tiled=True)  198 us
    psum x5, blocking collectives, over_axes(): return functools.reduce(lax.psum, axes, value)  51.4 us
    all_to_all x2, starting transfers between devices, from_everyone(): lax.all_to_all(jnp.broadcast_to(value[None], (length, *value.shape)), axi...  49.3 us
    all_gather x1, blocking collectives, on_device(): whole_rows = lax.all_gather(latents, TP, axis=1, tiled=True)  46.2 us
    all_gather x1, blocking collectives, on_device(): whole_rows = lax.all_gather(state_shard, TP, axis=1, tiled=True)  33.6 us
    all_to_all x2, waiting for transfers between devices, from_everyone(): lax.all_to_all(jnp.broadcast_to(value[None], (length, *value.shape)), axi...  29 us
  transfers between devices with their start and end apart: 6, of which 4 were waited for; matrix products, arithmetic and copies ran while one was open for 4% of the time, Pallas kernels for 0%

commit v1 on v0

v1 whole, which is shorter than its diff:
```python
import math

import jax
import jax.numpy as jnp
from jax import lax
from jax.experimental import pallas as pl
from jax.experimental.pallas import tpu as pltpu
from jax.sharding import Mesh
from jax.sharding import PartitionSpec as P

SEQ = ("seq_0", "seq_1")
TP = ("tp_0", "tp_1", "tp_2")
MESH = pl.DeviceIdType.MESH
F32, BF16 = jnp.float32, jnp.bfloat16
NX, NY, NZ = 4, 8, 4
ROWS, HALF = 128, 64
CHUNK, CHUNKS = 384, 8
WIDTH, INNER, HEAD = 3072, 1024, 128
EPS = 1e-6
KINETIC = 0.1
STEP = 0.125
EXP_SCALE = math.log2(math.e) / math.sqrt(HEAD)
MAX_COPIES = 192


def kernel(
    lengths_ref,
    t_index_ref,
    latents_hbm,
    mod_ref,
    wq_hbm,
    wk_hbm,
    wv_hbm,
    wo_hbm,
    q_gain_ref,
    k_gain_ref,
    ws_hbm,
    target_ref,
    student_ref,
    loss_ref,
    lat,
    half_in,
    wqkv,
    wo,
    ws,
    xbuf,
    wcols,
    qbuf,
    kvbuf,
    obuf,
    esend,
    erecv,
    abuf,
    pbuf,
    vbuf,
    v1buf,
    ssend,
    srecv,
    sx_send,
    sx_recv,
    sz_send,
    sz_recv,
    ubuf,
    acc_qkv,
    acc_o,
    lossbuf,
    local_sem,
    send_sem,
    recv_sem,
):
    z = lax.axis_index("seq_0")
    y = lax.axis_index("seq_1")
    x = lax.axis_index("tp_0")
    zh = lax.axis_index("tp_1")
    c = lax.axis_index("tp_2")
    other = 1 - c

    loads = [
        pltpu.make_async_copy(latents_hbm, lat, local_sem.at[0]),
        pltpu.make_async_copy(wq_hbm, wqkv.at[:, 0:HEAD], local_sem.at[1]),
        pltpu.make_async_copy(wk_hbm, wqkv.at[:, HEAD : 2 * HEAD], local_sem.at[2]),
        pltpu.make_async_copy(wv_hbm, wqkv.at[:, 2 * HEAD : 3 * HEAD], local_sem.at[3]),
        pltpu.make_async_copy(wo_hbm, wo, local_sem.at[4]),
        pltpu.make_async_copy(ws_hbm, ws, local_sem.at[5]),
    ]
    for load in loads:
        load.start()

    barrier = pltpu.get_barrier_semaphore()
    peers = [{"seq_1": lax.rem(y + d, NY)} for d in range(1, NY)]
    peers += [{"seq_0": lax.rem(z + d, NZ)} for d in range(1, NZ)]
    peers += [{"seq_0": lax.rem(z + d, NZ), "tp_1": 1 - zh} for d in range(NZ)]
    peers += [{"tp_0": lax.rem(x + d, NX)} for d in range(1, NX)]
    peers += [{"tp_0": lax.rem(x + d, NX), "tp_2": other} for d in range(NX)]
    for peer in peers:
        pl.semaphore_signal(barrier, inc=1, device_id=peer, device_id_type=MESH)
    pl.semaphore_wait(barrier, len(peers))

    count = [0]
    sends = []

    def slot():
        count[0] += 1
        assert count[0] <= MAX_COPIES
        return count[0] - 1

    def send(src, dst, k, **where):
        copy = pltpu.make_async_remote_copy(
            src_ref=src,
            dst_ref=dst,
            send_sem=send_sem.at[k],
            recv_sem=recv_sem.at[k],
            device_id=where,
            device_id_type=MESH,
        )
        copy.start()
        sends.append(copy)

    def arrived(dst, k, **where):
        pltpu.make_async_remote_copy(
            src_ref=dst,
            dst_ref=dst,
            send_sem=send_sem.at[k],
            recv_sem=recv_sem.at[k],
            device_id=where,
            device_id_type=MESH,
        ).wait_recv()

    def x_at(d):
        return lax.rem(x + d + NX, NX)

    def rows_of(which):
        return pl.ds(pl.multiple_of(which * HALF, HALF), HALF)

    def half_columns(value):
        return jnp.where(c == 0, value[:, 0:192], value[:, 192:384])

    first_length = lengths_ref[0]
    first_t = t_index_ref[0].astype(F32) * STEP
    second_t = t_index_ref[1].astype(F32) * STEP
    row_iota = lax.broadcasted_iota(jnp.int32, (ROWS, 1), 0)
    base = (z * NY + y) * ROWS
    in_first = (base + row_iota) < first_length
    start_times = jnp.where(in_first, first_t, second_t)

    loads[0].wait()
    k = slot()
    send(lat.at[rows_of(other), :], half_in, k, tp_2=other)
    arrived(half_in, k, tp_2=other)
    mine = lat[rows_of(c), :].astype(F32)
    theirs = half_in[...].astype(F32)
    left = jnp.where(c == 0, mine, theirs)
    right = jnp.where(c == 0, theirs, mine)
    own_chunk = 2 * x + zh
    xbuf[own_chunk, rows_of(c), :] = jnp.concatenate([left, right], axis=1).astype(BF16)

    def piece(chunk, which):
        return xbuf.at[chunk, rows_of(which), :]

    k_z = slot()
    send(piece(own_chunk, c), piece(own_chunk, c), k_z, tp_1=1 - zh)
    k_x = [[slot() for _ in range(1, NX)] for _ in range(2)]
    k_c = [slot() for _ in range(CHUNKS)]
    for d in range(1, NX):
        send(piece(own_chunk, c), piece(own_chunk, c), k_x[0][d - 1], tp_0=x_at(d))
    send(piece(own_chunk, c), piece(own_chunk, c), k_c[0], tp_2=other)
    arrivals = [own_chunk]
    for d in range(1, NX):
        chunk = 2 * x_at(-d) + zh
        arrived(piece(chunk, c), k_x[0][d - 1], tp_0=x_at(-d))
        send(piece(chunk, c), piece(chunk, c), k_c[d], tp_2=other)
        arrivals.append(chunk)
    far_chunk = 2 * x + 1 - zh
    arrived(piece(far_chunk, c), k_z, tp_1=1 - zh)
    for d in range(1, NX):
        send(piece(far_chunk, c), piece(far_chunk, c), k_x[1][d - 1], tp_0=x_at(d))
    send(piece(far_chunk, c), piece(far_chunk, c), k_c[NX], tp_2=other)
    arrivals.append(far_chunk)

    for load in loads[1:4]:
        load.wait()

    def project_chunk(number, chunk, state, times, squares):
        modulation = mod_ref[pl.ds(chunk, 1), :]
        squares = squares + jnp.sum(state * state, axis=1, keepdims=True)
        hidden = (state * (1.0 + times * modulation)).astype(BF16)
        weights = wqkv[pl.ds(pl.multiple_of(chunk * CHUNK, CHUNK), CHUNK), :]
        term = jnp.dot(hidden, weights, preferred_element_type=F32)
        if number == 0:
            acc_qkv[...] = term
        else:
            acc_qkv[...] += term
        return squares, hidden

    squares = jnp.zeros((ROWS, 1), F32)
    own_hidden = None

    def latents_chunk(number, squares):
        chunk = arrivals[number]
        arrived(piece(chunk, other), k_c[number], tp_2=other)
        return project_chunk(number, chunk, xbuf[chunk].astype(F32), start_times, squares)

    for number in range(NX + 1):
        squares, hidden = latents_chunk(number, squares)
        if number == 0:
            own_hidden = hidden
    for d in range(1, NX):
        chunk = 2 * x_at(-d) + 1 - zh
        arrived(piece(chunk, c), k_x[1][d - 1], tp_0=x_at(-d))
        send(piece(chunk, c), piece(chunk, c), k_c[NX + d], tp_2=other)
        arrivals.append(chunk)
    for number in range(NX + 1, CHUNKS):
        squares, hidden = latents_chunk(number, squares)

    def head_norm(value, gain):
        return (value * lax.rsqrt(jnp.mean(value * value, axis=1, keepdims=True) + EPS) * gain).astype(BF16)

    eye = lax.broadcasted_iota(jnp.int32, (ROWS, ROWS), 0) == lax.broadcasted_iota(
        jnp.int32, (ROWS, ROWS), 1
    )
    lane_iota = lax.broadcasted_iota(jnp.int32, (1, ROWS), 1)

    def attention(e, inverse, while_waiting):
        scaled = acc_qkv[...] * inverse
        qbuf[e, z] = head_norm(scaled[:, 0:HEAD], q_gain_ref[...])
        kvbuf[e, y, 0] = head_norm(scaled[:, HEAD : 2 * HEAD], k_gain_ref[...])
        kvbuf[e, y, 1] = scaled[:, 2 * HEAD : 3 * HEAD].astype(BF16)
        up, down = lax.rem(y + 1, NY), lax.rem(y + NY - 1, NY)
        k_ring = [[[slot(), slot()] for _ in range(4)] for _ in range(2)]
        k_q = [slot() for _ in range(1, NZ)]

        def part(owner, which):
            return kvbuf.at[e, owner, which]

        def pass_on(owner, which, direction, hop):
            target = up if direction == 0 else down
            send(part(owner, which), part(owner, which), k_ring[direction][hop][which], seq_1=target)

        for which in range(2):
            for direction in range(2):
                pass_on(y, which, direction, 0)
        for d in range(1, NZ):
            send(qbuf.at[e, z], qbuf.at[e, z], k_q[d - 1], seq_0=lax.rem(z + d, NZ))
        while_waiting[0]()

        def take(hop):
            owners = (lax.rem(y + NY - hop, NY), lax.rem(y + hop, NY))
            for which in range(2):
                for direction in range(2):
                    if hop == 4 and which != direction:
                        continue
                    source = down if direction == 0 else up
                    arrived(part(owners[direction], which), k_ring[direction][hop - 1][which], seq_1=source)
                    if hop < 3 or (hop == 3 and which == direction):
                        pass_on(owners[direction], which, direction, hop)
            return owners

        queries_from = [lax.rem(z + d, NZ) for d in range(NZ)]

        def block(owner, first):
            keys, values = kvbuf[e, owner, 0], kvbuf[e, owner, 1]
            both = jnp.concatenate([values, jnp.ones_like(values)], axis=1)
            key_first = ((z * NY + owner) * ROWS + lane_iota) < first_length
            for i in range(NZ):
                query_first = ((i * NY + y) * ROWS + row_iota) < first_length
                scores = lax.dot_general(
                    qbuf[e, i], keys, (((1,), (1,)), ((), ())), preferred_element_type=F32
                )
                same = jnp.logical_xor(query_first, jnp.logical_not(key_first))
                weights = jnp.where(same, jnp.exp2(scores * EXP_SCALE), 0.0).astype(BF16)
                term = jnp.dot(weights, both, preferred_element_type=F32)
                if first:
                    acc_o[i] = term
                else:
                    acc_o[i] += term

        around = take(1)
        for d in range(1, NZ):
            source = lax.rem(z + NZ - d, NZ)
            arrived(qbuf.at[e, source], k_q[d - 1], seq_0=source)
        block(y, True)
        for owner in around:
            block(owner, False)
        for hop in (2, 3):
            for owner in take(hop):
                block(owner, False)
        block(take(4)[0], False)

        k_e = [slot() for _ in range(1, NZ)]
        head16 = lax.broadcasted_iota(jnp.int32, (16, ROWS), 0)

        for i in range(NZ):
            product = acc_o[i]
            total = jnp.sum(jnp.where(eye, product[:, HEAD:], 0.0), axis=0, keepdims=True)
            high = total.astype(BF16).astype(F32)
            low = total - high
            esend[e, i, 0:ROWS, :] = product[:, 0:HEAD].astype(BF16)
            esend[e, i, ROWS : ROWS + 16, :] = jnp.where(
                head16 == 0, high, jnp.where(head16 == 1, low, 0.0)
            ).astype(BF16)
        for d in range(1, NZ):
            target = lax.rem(z + d, NZ)
            send(esend.at[e, target], erecv.at[e, d - 1], k_e[d - 1], seq_0=target)
        while_waiting[1]()

        mixed = esend[e, z].astype(F32)
        for d in range(1, NZ):
            arrived(erecv.at[e, d - 1], k_e[d - 1], seq_0=lax.rem(z + NZ - d, NZ))
            mixed = mixed + erecv[e, d - 1].astype(F32)
        total = mixed[ROWS : ROWS + 1, :] + mixed[ROWS + 1 : ROWS + 2, :]
        column = jnp.sum(jnp.where(eye, total, 0.0), axis=1, keepdims=True)
        return (mixed[0:ROWS, :] / column).astype(BF16)

    def velocity(e, attended, while_waiting):
        abuf[e, 2 * x + c] = attended
        k_a = [[slot(), slot()] for _ in range(NX)]
        for d in range(NX):
            for flip in range(2):
                if d == 0 and flip == 0:
                    continue
                send(
                    abuf.at[e, 2 * x + c],
                    abuf.at[e, 2 * x + c],
                    k_a[d][flip],
                    tp_0=x_at(d),
                    tp_2=c if flip == 0 else other,
                )
        while_waiting[0]()
        for d in range(NX):
            for flip in range(2):
                if d == 0 and flip == 0:
                    continue
                core = c if flip == 0 else other
                arrived(abuf.at[e, 2 * x_at(-d) + core], k_a[d][flip], tp_0=x_at(-d), tp_2=core)
        heads = jnp.concatenate([abuf[e, i] for i in range(CHUNKS)], axis=1)
        partial = jnp.dot(heads, wcols[...].reshape(INNER, CHUNK), preferred_element_type=F32)
        pbuf[e, 0] = partial.astype(BF16)
        k_p = slot()
        send(pbuf.at[e, 0], pbuf.at[e, 1], k_p, tp_1=1 - zh)
        while_waiting[1]()
        arrived(pbuf.at[e, 1], k_p, tp_1=1 - zh)
        return (pbuf[e, 0].astype(F32) + pbuf[e, 1].astype(F32)).astype(BF16)

    k_w = [[slot(), slot()] for _ in range(NX)]
    k_sc = slot()
    k_sx = [slot() for _ in range(1, NX)]
    k_sz = slot()
    k_su = slot()
    inverse = lax.rsqrt(squares * (1.0 / WIDTH) + EPS)

    def send_columns():
        loads[4].wait()
        for d in range(NX):
            for flip in range(2):
                if d == 0 and flip == 0:
                    continue
                core = c if flip == 0 else other
                columns = pl.ds(pl.multiple_of((2 * x_at(d) + core) * CHUNK, CHUNK), CHUNK)
                send(wo.at[:, columns], wcols.at[2 * x + c], k_w[d][flip], tp_0=x_at(d), tp_2=core)
        wcols[2 * x + c] = wo[:, pl.ds(pl.multiple_of((2 * x + c) * CHUNK, CHUNK), CHUNK)]
        loads[5].wait()
        rows = half_columns(own_hidden.astype(F32)).astype(BF16)
        for j in range(CHUNKS):
            product = jnp.dot(rows, ws[:, j * CHUNK : (j + 1) * CHUNK], preferred_element_type=F32) * inverse
            ssend[0, j] = product[0:HALF].astype(BF16)
            ssend[1, j] = product[HALF:ROWS].astype(BF16)
        send(ssend.at[other], srecv, k_sc, tp_2=other)

    def student_x():
        arrived(srecv, k_sc, tp_2=other)
        for j in range(CHUNKS):
            sx_send[j] = (ssend[c, j].astype(F32) + srecv[j].astype(F32)).astype(BF16)
        for d in range(1, NX):
            send(sx_send.at[pl.ds(2 * x_at(d), 2)], sx_recv.at[d - 1], k_sx[d - 1], tp_0=x_at(d))

    def student_z():
        total = sx_send[pl.ds(2 * x, 2)].astype(F32)
        for d in range(1, NX):
            arrived(sx_recv.at[d - 1], k_sx[d - 1], tp_0=x_at(-d))
            total = total + sx_recv[d - 1].astype(F32)
        sz_send[...] = total.astype(BF16)
        send(sz_send.at[1 - zh], sz_recv, k_sz, tp_1=1 - zh)

    def columns_here():
        for d in range(NX):
            for flip in range(2):
                if d == 0 and flip == 0:
                    continue
                core = c if flip == 0 else other
                arrived(wcols.at[2 * x_at(-d) + core], k_w[d][flip], tp_0=x_at(-d), tp_2=core)

    def student_core():
        arrived(sz_recv, k_sz, tp_1=1 - zh)
        ubuf[c] = (sz_send[zh].astype(F32) + sz_recv[...].astype(F32)).astype(BF16)
        send(ubuf.at[c], ubuf.at[c], k_su, tp_2=other)

    def nothing():
        pass

    attended = attention(0, inverse, (send_columns, student_x))
    first = velocity(0, attended, (columns_here, student_z))

    own_slot = 2 * x + c
    vbuf[own_slot] = first
    k_vx = [slot() for _ in range(1, NX)]
    k_vc = [slot() for _ in range(NX)]
    for d in range(1, NX):
        send(vbuf.at[own_slot], vbuf.at[own_slot], k_vx[d - 1], tp_0=x_at(d))
    send(vbuf.at[own_slot], vbuf.at[own_slot], k_vc[0], tp_2=other)
    squares = jnp.zeros((ROWS, 1), F32)
    times = start_times + STEP

    def state_chunk(number, chunk, squares):
        state = (xbuf[chunk].astype(F32) + STEP * vbuf[chunk].astype(F32)).astype(BF16)
        return project_chunk(number, chunk, state.astype(F32), times, squares)[0]

    squares = state_chunk(0, own_slot, squares)
    arrived(vbuf.at[2 * x + other], k_vc[0], tp_2=other)
    squares = state_chunk(1, 2 * x + other, squares)
    student_core()
    for d in range(1, NX):
        theirs = 2 * x_at(-d) + c
        arrived(vbuf.at[theirs], k_vx[d - 1], tp_0=x_at(-d))
        send(vbuf.at[theirs], vbuf.at[theirs], k_vc[d], tp_2=other)
        squares = state_chunk(2 * d, theirs, squares)
        if d > 1:
            last = 2 * x_at(1 - d) + other
            arrived(vbuf.at[last], k_vc[d - 1], tp_2=other)
            squares = state_chunk(2 * d - 1, last, squares)
    last = 2 * x_at(1 - NX) + other
    arrived(vbuf.at[last], k_vc[NX - 1], tp_2=other)
    squares = state_chunk(7, last, squares)

    inverse = lax.rsqrt(squares * (1.0 / WIDTH) + EPS)
    attended = attention(1, inverse, (nothing, nothing))
    second = velocity(1, attended, (nothing, nothing))
    v1buf[c] = second
    k_v1 = slot()
    send(v1buf.at[c], v1buf.at[c], k_v1, tp_2=other)

    arrived(ubuf.at[other], k_su, tp_2=other)
    student = half_columns(jnp.concatenate([ubuf[0], ubuf[1]], axis=0).astype(F32))
    student_ref[...] = student.astype(BF16)
    start_velocity = half_columns(vbuf[own_chunk].astype(F32))
    arrived(v1buf.at[other], k_v1, tp_2=other)
    end_velocity = half_columns(v1buf[zh].astype(F32))
    target = (0.5 * (start_velocity + end_velocity)).astype(BF16)
    target_ref[...] = target
    residual = student - target.astype(F32)
    per_token = jnp.sum(residual * residual + KINETIC * (student * student), axis=1, keepdims=True)
    first_sum = jnp.sum(jnp.where(in_first, per_token, 0.0), axis=0, keepdims=True)
    second_sum = jnp.sum(jnp.where(in_first, 0.0, per_token), axis=0, keepdims=True)
    lanes = lax.broadcasted_iota(jnp.int32, (8, ROWS), 1)
    sums = jnp.where(lanes == 0, first_sum, jnp.where(lanes == 1, second_sum, 0.0))

    def exchanged(stage, own, others, sums):
        lossbuf[stage, own] = sums
        numbers = [slot() for _ in others]
        for number, (where, target, source) in zip(numbers, others):
            send(lossbuf.at[stage, own], lossbuf.at[stage, own], number, **where(target))
        for number, (where, target, source) in zip(numbers, others):
            index = source[0]
            arrived(lossbuf.at[stage, index], number, **where(source))
        total = lossbuf[stage, 0]
        for i in range(1, 8):
            total = total + lossbuf[stage, i]
        return total

    def over_x(place):
        return {"tp_0": place[1], "tp_2": place[2]}

    def over_y(place):
        return {"seq_1": place[0]}

    def over_z(place):
        return {"tp_1": place[1], "seq_0": place[2]}

    x_others = []
    for d in range(NX):
        for core in (c, other):
            if d == 0 and core is c:
                continue
            x_others.append(
                (over_x, (None, x_at(d), core), (2 * x_at(-d) + core, x_at(-d), core))
            )
    sums = exchanged(0, 2 * x + c, x_others, sums)
    y_others = [
        (over_y, (lax.rem(y + d, NY),), (lax.rem(y + NY - d, NY),)) for d in range(1, NY)
    ]
    sums = exchanged(1, y, y_others, sums)
    z_others = []
    for d in range(NZ):
        for half in (zh, 1 - zh):
            if d == 0 and half is zh:
                continue
            ahead, behind = lax.rem(z + d, NZ), lax.rem(z + NZ - d, NZ)
            z_others.append((over_z, (None, half, ahead), (half * NZ + behind, half, behind)))
    sums = exchanged(2, zh * NZ + z, z_others, sums)
    scale = jnp.where(
        lanes == 0,
        1.0 / (lengths_ref[0].astype(F32) * WIDTH),
        1.0 / (lengths_ref[1].astype(F32) * WIDTH),
    )
    loss_ref[0, 0] = 0.5 * jnp.sum((sums * scale)[0:1, :])

    for copy in sends:
        copy.wait_send()


def on_device(
    latents,
    lengths,
    t_index,
    mod_scale,
    q_weight,
    k_weight,
    v_weight,
    out_weight,
    q_gain,
    k_gain,
    student_weight,
):
    smem = pl.BlockSpec(memory_space=pltpu.SMEM)
    vmem = pl.BlockSpec(memory_space=pltpu.VMEM)
    anywhere = pl.BlockSpec(memory_space=pl.ANY)
    target, student, loss = pl.pallas_call(
        kernel,
        out_shape=(
            jax.ShapeDtypeStruct((ROWS, 192), BF16),
            jax.ShapeDtypeStruct((ROWS, 192), BF16),
            jax.ShapeDtypeStruct((1, 1), F32),
        ),
        in_specs=[smem, smem, anywhere, vmem, anywhere, anywhere, anywhere, anywhere, vmem, vmem, anywhere],
        out_specs=(vmem, vmem, smem),
        scratch_shapes=[
            pltpu.VMEM((ROWS, 192), BF16),
            pltpu.VMEM((HALF, 192), BF16),
            pltpu.VMEM((WIDTH, CHUNK), BF16),
            pltpu.VMEM((ROWS, WIDTH), BF16),
            pltpu.VMEM((192, WIDTH), BF16),
            pltpu.VMEM((CHUNKS, ROWS, CHUNK), BF16),
            pltpu.VMEM((CHUNKS, ROWS, CHUNK), BF16),
            pltpu.VMEM((2, NZ, ROWS, HEAD), BF16),
            pltpu.VMEM((2, NY, 2, ROWS, HEAD), BF16),
            pltpu.VMEM((8, 128), F32),
            pltpu.VMEM((2, NZ, ROWS + 16, HEAD), BF16),
            pltpu.VMEM((2, NZ - 1, ROWS + 16, HEAD), BF16),
            pltpu.VMEM((2, CHUNKS, ROWS, HEAD), BF16),
            pltpu.VMEM((2, 2, ROWS, CHUNK), BF16),
            pltpu.VMEM((CHUNKS, ROWS, CHUNK), BF16),
            pltpu.VMEM((2, ROWS, CHUNK), BF16),
            pltpu.VMEM((2, CHUNKS, HALF, CHUNK), BF16),
            pltpu.VMEM((CHUNKS, HALF, CHUNK), BF16),
            pltpu.VMEM((CHUNKS, HALF, CHUNK), BF16),
            pltpu.VMEM((NX - 1, 2, HALF, CHUNK), BF16),
            pltpu.VMEM((2, HALF, CHUNK), BF16),
            pltpu.VMEM((HALF, CHUNK), BF16),
            pltpu.VMEM((2, HALF, CHUNK), BF16),
            pltpu.VMEM((ROWS, CHUNK), F32),
            pltpu.VMEM((NZ, ROWS, 2 * HEAD), F32),
            pltpu.VMEM((3, 8, 8, 128), F32),
            pltpu.SemaphoreType.DMA((6,)),
            pltpu.SemaphoreType.DMA((MAX_COPIES,)),
            pltpu.SemaphoreType.DMA((MAX_COPIES,)),
        ],
        compiler_params=pltpu.CompilerParams(
            collective_id=0, has_side_effects=True, vmem_limit_bytes=48 * 1024 * 1024
        ),
    )(
        lengths,
        t_index,
        latents,
        mod_scale.reshape(CHUNKS, CHUNK),
        q_weight,
        k_weight,
        v_weight,
        out_weight,
        q_gain.reshape(1, HEAD),
        k_gain.reshape(1, HEAD),
        student_weight,
    )
    return (target, student, loss.reshape(()))


def solution(mesh):
    torus = Mesh(
        mesh.devices.reshape(4, 8, 4, 2, 2), ("seq_0", "seq_1", "tp_0", "tp_1", "tp_2")
    )
    in_specs = (
        P(SEQ, TP),
        P(),
        P(),
        P(),
        P(None, TP),
        P(None, TP),
        P(None, TP),
        P(TP, None),
        P(),
        P(),
        P(TP, None),
    )
    out_specs = (P(SEQ, TP), P(SEQ, TP), P())
    return jax.shard_map(
        on_device, mesh=torus, in_specs=in_specs, out_specs=out_specs, check_vma=False
    )
```

time: 473 us -> 130 us (0.27)
  waiting for transfers between devices: 227 us -> 0 us
  blocking collectives: 131 us -> 0 us
  Pallas kernels: 0 us -> 116 us
  starting transfers between devices: 62.3 us -> 0 us
  matrix products: 18.5 us -> 0 us
  between operations: 16.1 us -> 2.42 us
  other arithmetic: 10.8 us -> 0 us
  local copies, waits for them, and re-layouts: 5.83 us -> 11.5 us
    all_gather x2 -> x0, waiting for transfers between devices: 198 us -> none  [in_one_piece(): whole = lax.all_gather(both, axis, axis=dim, tiled=True)]
    pallas_call x0 -> x1, Pallas kernels: none -> 116 us  [on_device(): pl.pallas_call(kernel, out_shape=(jax.ShapeDtypeStruct((ROWS, 192), BF16)...]
    all_gather x2 -> x0, blocking collectives: 79.8 us -> none  [the longest x1 46.2 us: on_device(): whole_rows = lax.all_gather(latents, TP, axis=1, tiled=True)]
    all_to_all x4 -> x0, starting transfers between devices: 62.2 us -> none  [the longest x2 49.3 us: from_everyone(): lax.all_to_all(jnp.broadcast_to(value[None], (length, *value.shape)), axi...]
    psum x5 -> x0, blocking collectives: 51.4 us -> none  [over_axes(): return functools.reduce(lax.psum, axes, value)]
    all_to_all x4 -> x0, waiting for transfers between devices: 29 us -> none  [the longest x2 29 us: from_everyone(): lax.all_to_all(jnp.broadcast_to(value[None], (length, *value.shape)), axi...]
    dot_general x13 -> x0, matrix products: 18.5 us -> none  [the longest x3 4.97 us: grouped_columns(): jnp.einsum('tng,ngd->tnd', left_groups, right_groups, preferred_element_t...]
    unnamed x24 -> x21, local copies, waits for them, and re-layouts: 3.77 us -> 10.8 us
  transfers between devices with their start and end apart: 6 -> 0, of which waited for: 4 -> 0; matrix products, arithmetic and copies ran while one was open for 4% -> 0% of each run, Pallas kernels for 0% -> 0%
where the time goes in v1:
time: 130 us
  Pallas kernels  116 us (89%)
  local copies, waits for them, and re-layouts  11.5 us (9%)
  between operations  2.42 us (2%)
    pallas_call x1, Pallas kernels, on_device(): pl.pallas_call(kernel, out_shape=(jax.ShapeDtypeStruct((ROWS, 192), BF16)...  116 us
    unnamed x21, local copies, waits for them, and re-layouts  10.8 us

profile of v1, /device:TPU:1, one launch (start us, length us, event | category | flops | bytes accessed | tf_op | source)
XLA Modules:
  0.0 129.7 jit_solution(3915031690691172258)
XLA Ops:
  0.6 0.7 reshape.18.mod_ref
  1.3 0.9 copy.14.latents_hbm
  2.2 0.0 copy-start
  2.3 1.3 copy-done
  3.5 0.0 copy-start.1
  3.5 1.1 copy-done.1
  4.7 0.0 copy-start.2
  4.7 1.1 copy-done.2
  5.8 0.0 copy-start.3
  5.8 1.1 copy-done.3
  6.9 0.0 copy-start.4
  6.9 1.1 copy-done.4
  8.1 0.0 copy-start.5
  8.1 0.7 copy-done.5
  8.7 0.0 copy-start.6
  8.7 0.7 copy-done.6
  9.4 0.0 copy-start.7
  9.4 0.7 copy-done.7
  10.0 0.0 copy-start.8
  10.0 0.7 copy-done.8
  10.7 115.8 %shard_map.130 = (bf16[128,192]{1,0:T(8,128)(2,1)S(1)}, bf16[128,192]{1,0:T(8,128)(2,1)S(1)}, f32[1,1]{1,0:T(1,128)}) custom-call(s32[2]{0:T(128)S(1)} %copy-done.5, s32[2]{0:T(128)S(1)} %copy-done.6, bf16[128,192]{1,0:T(8,128)(2,1)S(1)} %copy.14.latents_hbm, f32[8,384]{1,0:T(8,128)S(1)} %reshape.18.mod_ref, bf16[3072,128]{1,0:T(8,128)(2,1)S(1)} %copy-done.1, ...), custom_call_target="tpu_custom_call" | custom-call | tf_op jit(solution)/shard_map/pallas_call | solution.py:526
  126.5 0.7 copy.15
  127.3 0.7 copy.16
Async XLA Ops:
  2.2 1.3 copy-start
  3.5 1.1 copy-start.1
  4.7 1.1 copy-start.2
  5.8 1.1 copy-start.3
  6.9 1.1 copy-start.4
  8.1 0.7 copy-start.5
  8.7 0.7 copy-start.6
  9.4 0.7 copy-start.7
  10.0 0.7 copy-start.8

commit v2 on v1

--- a/solution.py
+++ b/solution.py
@@ -20,7 +20,8 @@
 KINETIC = 0.1
 STEP = 0.125
 EXP_SCALE = math.log2(math.e) / math.sqrt(HEAD)
-MAX_COPIES = 192
+MAX_COPIES = 224
+VMEM_LIMIT = 67043328
 
 
 def kernel(
@@ -38,8 +39,7 @@
     target_ref,
     student_ref,
     loss_ref,
-    lat,
-    half_in,
+    xt,
     wqkv,
     wo,
     ws,
@@ -76,7 +76,7 @@
     other = 1 - c
 
     loads = [
-        pltpu.make_async_copy(latents_hbm, lat, local_sem.at[0]),
+        pltpu.make_async_copy(latents_hbm, xt.at[2 * x + zh, pl.ds(pl.multiple_of(c * 192, 192), 192), :], local_sem.at[0]),
         pltpu.make_async_copy(wq_hbm, wqkv.at[:, 0:HEAD], local_sem.at[1]),
         pltpu.make_async_copy(wk_hbm, wqkv.at[:, HEAD : 2 * HEAD], local_sem.at[2]),
         pltpu.make_async_copy(wv_hbm, wqkv.at[:, 2 * HEAD : 3 * HEAD], local_sem.at[3]),
@@ -94,6 +94,7 @@
     peers += [{"tp_0": lax.rem(x + d, NX), "tp_2": other} for d in range(NX)]
     for peer in peers:
         pl.semaphore_signal(barrier, inc=1, device_id=peer, device_id_type=MESH)
+    loads[0].wait()
     pl.semaphore_wait(barrier, len(peers))
 
     count = [0]
@@ -104,8 +105,8 @@
         assert count[0] <= MAX_COPIES
         return count[0] - 1
 
-    def send(src, dst, k, **where):
-        copy = pltpu.make_async_remote_copy(
+    def remote(src, dst, k, **where):
+        return pltpu.make_async_remote_copy(
             src_ref=src,
             dst_ref=dst,
             send_sem=send_sem.at[k],
@@ -113,18 +114,14 @@
             device_id=where,
             device_id_type=MESH,
         )
+
+    def send(src, dst, k, **where):
+        copy = remote(src, dst, k, **where)
         copy.start()
         sends.append(copy)
 
     def arrived(dst, k, **where):
-        pltpu.make_async_remote_copy(
-            src_ref=dst,
-            dst_ref=dst,
-            send_sem=send_sem.at[k],
-            recv_sem=recv_sem.at[k],
-            device_id=where,
-            device_id_type=MESH,
-        ).wait_recv()
+        remote(dst, dst, k, **where).wait_recv()
 
     def x_at(d):
         return lax.rem(x + d + NX, NX)
@@ -143,19 +140,10 @@
     in_first = (base + row_iota) < first_length
     start_times = jnp.where(in_first, first_t, second_t)
 
-    loads[0].wait()
-    k = slot()
-    send(lat.at[rows_of(other), :], half_in, k, tp_2=other)
-    arrived(half_in, k, tp_2=other)
-    mine = lat[rows_of(c), :].astype(F32)
-    theirs = half_in[...].astype(F32)
-    left = jnp.where(c == 0, mine, theirs)
-    right = jnp.where(c == 0, theirs, mine)
     own_chunk = 2 * x + zh
-    xbuf[own_chunk, rows_of(c), :] = jnp.concatenate([left, right], axis=1).astype(BF16)
 
     def piece(chunk, which):
-        return xbuf.at[chunk, rows_of(which), :]
+        return xt.at[chunk, pl.ds(pl.multiple_of(which * 192, 192), 192), :]
 
     k_z = slot()
     send(piece(own_chunk, c), piece(own_chunk, c), k_z, tp_1=1 - zh)
@@ -181,7 +169,7 @@
         load.wait()
 
     def project_chunk(number, chunk, state, times, squares):
-        modulation = mod_ref[pl.ds(chunk, 1), :]
+        modulation = mod_ref[:, pl.ds(pl.multiple_of(chunk * CHUNK, CHUNK), CHUNK)]
         squares = squares + jnp.sum(state * state, axis=1, keepdims=True)
         hidden = (state * (1.0 + times * modulation)).astype(BF16)
         weights = wqkv[pl.ds(pl.multiple_of(chunk * CHUNK, CHUNK), CHUNK), :]
@@ -198,7 +186,9 @@
     def latents_chunk(number, squares):
         chunk = arrivals[number]
         arrived(piece(chunk, other), k_c[number], tp_2=other)
-        return project_chunk(number, chunk, xbuf[chunk].astype(F32), start_times, squares)
+        state = xt[chunk].T
+        xbuf[chunk] = state
+        return project_chunk(number, chunk, state.astype(F32), start_times, squares)
 
     for number in range(NX + 1):
         squares, hidden = latents_chunk(number, squares)
@@ -311,35 +301,39 @@
         column = jnp.sum(jnp.where(eye, total, 0.0), axis=1, keepdims=True)
         return (mixed[0:ROWS, :] / column).astype(BF16)
 
-    def velocity(e, attended, while_waiting):
-        abuf[e, 2 * x + c] = attended
-        k_a = [[slot(), slot()] for _ in range(NX)]
-        for d in range(NX):
-            for flip in range(2):
-                if d == 0 and flip == 0:
-                    continue
-                send(
-                    abuf.at[e, 2 * x + c],
-                    abuf.at[e, 2 * x + c],
-                    k_a[d][flip],
-                    tp_0=x_at(d),
-                    tp_2=c if flip == 0 else other,
-                )
-        while_waiting[0]()
-        for d in range(NX):
-            for flip in range(2):
-                if d == 0 and flip == 0:
-                    continue
-                core = c if flip == 0 else other
-                arrived(abuf.at[e, 2 * x_at(-d) + core], k_a[d][flip], tp_0=x_at(-d), tp_2=core)
-        heads = jnp.concatenate([abuf[e, i] for i in range(CHUNKS)], axis=1)
-        partial = jnp.dot(heads, wcols[...].reshape(INNER, CHUNK), preferred_element_type=F32)
-        pbuf[e, 0] = partial.astype(BF16)
-        k_p = slot()
-        send(pbuf.at[e, 0], pbuf.at[e, 1], k_p, tp_1=1 - zh)
-        while_waiting[1]()
-        arrived(pbuf.at[e, 1], k_p, tp_1=1 - zh)
-        return (pbuf[e, 0].astype(F32) + pbuf[e, 1].astype(F32)).astype(BF16)
+    def partial_velocity(e, attended, while_waiting, hand_on):
+        own = 2 * x + c
+        k_a = [[[slot(), slot()] for _ in range(NX)] for _ in range(2)]
+        for h in range(2):
+            abuf[e, h, own] = attended[h * HALF : (h + 1) * HALF]
+            for d in range(NX):
+                for flip in range(2):
+                    if d == 0 and flip == 0:
+                        continue
+                    send(
+                        abuf.at[e, h, own],
+                        abuf.at[e, h, own],
+                        k_a[h][d][flip],
+                        tp_0=x_at(d),
+                        tp_2=c if flip == 0 else other,
+                    )
+        while_waiting()
+        for h in range(2):
+            for d in range(NX):
+                for flip in range(2):
+                    if d == 0 and flip == 0:
+                        continue
+                    core = c if flip == 0 else other
+                    arrived(
+                        abuf.at[e, h, 2 * x_at(-d) + core], k_a[h][d][flip], tp_0=x_at(-d), tp_2=core
+                    )
+            heads = jnp.concatenate([abuf[e, h, i] for i in range(CHUNKS)], axis=1)
+            partial = jnp.dot(heads, wcols[...].reshape(INNER, CHUNK), preferred_element_type=F32)
+            pbuf[e, 0, h] = partial.astype(BF16)
+            hand_on(h)
+
+    def both_partials(e, h):
+        return (pbuf[e, 0, h].astype(F32) + pbuf[e, 1, h].astype(F32)).astype(BF16)
 
     k_w = [[slot(), slot()] for _ in range(NX)]
     k_sc = slot()
@@ -398,15 +392,27 @@
         pass
 
     attended = attention(0, inverse, (send_columns, student_x))
-    first = velocity(0, attended, (columns_here, student_z))
+    k_p = [[slot(), slot()] for _ in range(2)]
+
+    def to_partner(h):
+        send(pbuf.at[0, 0, h], pbuf.at[0, 1, h], k_p[0][h], tp_1=1 - zh)
+
+    partial_velocity(0, attended, columns_here, to_partner)
+    student_z()
 
     own_slot = 2 * x + c
-    vbuf[own_slot] = first
-    k_vx = [slot() for _ in range(1, NX)]
-    k_vc = [slot() for _ in range(NX)]
-    for d in range(1, NX):
-        send(vbuf.at[own_slot], vbuf.at[own_slot], k_vx[d - 1], tp_0=x_at(d))
-    send(vbuf.at[own_slot], vbuf.at[own_slot], k_vc[0], tp_2=other)
+    k_vx = [[slot() for _ in range(1, NX)] for _ in range(2)]
+    k_vc = [[slot() for _ in range(NX)] for _ in range(2)]
+
+    def vpart(chunk, h):
+        return vbuf.at[chunk, h * HALF : (h + 1) * HALF, :]
+
+    for h in range(2):
+        arrived(pbuf.at[0, 1, h], k_p[0][h], tp_1=1 - zh)
+        vbuf[own_slot, h * HALF : (h + 1) * HALF, :] = both_partials(0, h)
+        for d in range(1, NX):
+            send(vpart(own_slot, h), vpart(own_slot, h), k_vx[h][d - 1], tp_0=x_at(d))
+        send(vpart(own_slot, h), vpart(own_slot, h), k_vc[h][0], tp_2=other)
     squares = jnp.zeros((ROWS, 1), F32)
     times = start_times + STEP
 
@@ -415,42 +421,74 @@
         return project_chunk(number, chunk, state.astype(F32), times, squares)[0]
 
     squares = state_chunk(0, own_slot, squares)
-    arrived(vbuf.at[2 * x + other], k_vc[0], tp_2=other)
+    for h in range(2):
+        arrived(vpart(2 * x + other, h), k_vc[h][0], tp_2=other)
     squares = state_chunk(1, 2 * x + other, squares)
     student_core()
+    for h in range(2):
+        for d in range(1, NX):
+            theirs = 2 * x_at(-d) + c
+            arrived(vpart(theirs, h), k_vx[h][d - 1], tp_0=x_at(-d))
+            send(vpart(theirs, h), vpart(theirs, h), k_vc[h][d], tp_2=other)
     for d in range(1, NX):
-        theirs = 2 * x_at(-d) + c
-        arrived(vbuf.at[theirs], k_vx[d - 1], tp_0=x_at(-d))
-        send(vbuf.at[theirs], vbuf.at[theirs], k_vc[d], tp_2=other)
-        squares = state_chunk(2 * d, theirs, squares)
-        if d > 1:
-            last = 2 * x_at(1 - d) + other
-            arrived(vbuf.at[last], k_vc[d - 1], tp_2=other)
-            squares = state_chunk(2 * d - 1, last, squares)
-    last = 2 * x_at(1 - NX) + other
-    arrived(vbuf.at[last], k_vc[NX - 1], tp_2=other)
-    squares = state_chunk(7, last, squares)
+        squares = state_chunk(2 * d, 2 * x_at(-d) + c, squares)
+    for d in range(1, NX):
+        last = 2 * x_at(-d) + other
+        for h in range(2):
+            arrived(vpart(last, h), k_vc[h][d], tp_2=other)
+        squares = state_chunk(2 * d + 1, last, squares)
 
     inverse = lax.rsqrt(squares * (1.0 / WIDTH) + EPS)
     attended = attention(1, inverse, (nothing, nothing))
-    second = velocity(1, attended, (nothing, nothing))
-    v1buf[c] = second
-    k_v1 = slot()
-    send(v1buf.at[c], v1buf.at[c], k_v1, tp_2=other)
+
+    adds, helps = c == zh, c != zh
+    k_v1 = [slot(), slot()]
+
+    def partner_copy(h):
+        return remote(pbuf.at[1, 0, h], pbuf.at[1, 1, h], k_p[1][h], tp_1=1 - zh)
+
+    def sibling_copy(h):
+        part = v1buf.at[h * HALF : (h + 1) * HALF, :]
+        return remote(part, part, k_v1[h], tp_2=other)
+
+    def to_partner_if_needed(h):
+        @pl.when(helps)
+        def _():
+            partner_copy(h).start()
+
+    partial_velocity(1, attended, nothing, to_partner_if_needed)
+
+    @pl.when(adds)
+    def _():
+        for h in range(2):
+            partner_copy(h).wait_recv()
+            v1buf[h * HALF : (h + 1) * HALF, :] = both_partials(1, h)
+            sibling_copy(h).start()
 
     arrived(ubuf.at[other], k_su, tp_2=other)
     student = half_columns(jnp.concatenate([ubuf[0], ubuf[1]], axis=0).astype(F32))
-    student_ref[...] = student.astype(BF16)
+    student_ref[...] = student.T.astype(BF16)
     start_velocity = half_columns(vbuf[own_chunk].astype(F32))
-    arrived(v1buf.at[other], k_v1, tp_2=other)
-    end_velocity = half_columns(v1buf[zh].astype(F32))
-    target = (0.5 * (start_velocity + end_velocity)).astype(BF16)
-    target_ref[...] = target
-    residual = student - target.astype(F32)
+
+    @pl.when(helps)
+    def _():
+        for h in range(2):
+            sibling_copy(h).wait_recv()
+            partner_copy(h).wait_send()
+
+    @pl.when(adds)
+    def _():
+        for h in range(2):
+            sibling_copy(h).wait_send()
+
+    end_velocity = half_columns(v1buf[...].astype(F32))
+    target = (0.5 * (start_velocity + end_velocity)).astype(BF16).astype(F32)
+    target_ref[...] = target.T.astype(BF16)
+    residual = student - target
     per_token = jnp.sum(residual * residual + KINETIC * (student * student), axis=1, keepdims=True)
     first_sum = jnp.sum(jnp.where(in_first, per_token, 0.0), axis=0, keepdims=True)
     second_sum = jnp.sum(jnp.where(in_first, 0.0, per_token), axis=0, keepdims=True)
-    lanes = lax.broadcasted_iota(jnp.int32, (8, ROWS), 1)
+    lanes = lane_iota
     sums = jnp.where(lanes == 0, first_sum, jnp.where(lanes == 1, second_sum, 0.0))
 
     def exchanged(stage, own, others, sums):
@@ -501,7 +539,7 @@
         1.0 / (lengths_ref[0].astype(F32) * WIDTH),
         1.0 / (lengths_ref[1].astype(F32) * WIDTH),
     )
-    loss_ref[0, 0] = 0.5 * jnp.sum((sums * scale)[0:1, :])
+    loss_ref[0, 0] = 0.5 * jnp.sum(sums * scale)
 
     for copy in sends:
         copy.wait_send()
@@ -526,15 +564,14 @@
     target, student, loss = pl.pallas_call(
         kernel,
         out_shape=(
-            jax.ShapeDtypeStruct((ROWS, 192), BF16),
-            jax.ShapeDtypeStruct((ROWS, 192), BF16),
+            jax.ShapeDtypeStruct((192, ROWS), BF16),
+            jax.ShapeDtypeStruct((192, ROWS), BF16),
             jax.ShapeDtypeStruct((1, 1), F32),
         ),
         in_specs=[smem, smem, anywhere, vmem, anywhere, anywhere, anywhere, anywhere, vmem, vmem, anywhere],
         out_specs=(vmem, vmem, smem),
         scratch_shapes=[
-            pltpu.VMEM((ROWS, 192), BF16),
-            pltpu.VMEM((HALF, 192), BF16),
+            pltpu.VMEM((CHUNKS, CHUNK, ROWS), BF16),
             pltpu.VMEM((WIDTH, CHUNK), BF16),
             pltpu.VMEM((ROWS, WIDTH), BF16),
             pltpu.VMEM((192, WIDTH), BF16),
@@ -545,10 +582,10 @@
             pltpu.VMEM((8, 128), F32),
             pltpu.VMEM((2, NZ, ROWS + 16, HEAD), BF16),
             pltpu.VMEM((2, NZ - 1, ROWS + 16, HEAD), BF16),
-            pltpu.VMEM((2, CHUNKS, ROWS, HEAD), BF16),
-            pltpu.VMEM((2, 2, ROWS, CHUNK), BF16),
+            pltpu.VMEM((2, 2, CHUNKS, HALF, HEAD), BF16),
+            pltpu.VMEM((2, 2, 2, HALF, CHUNK), BF16),
             pltpu.VMEM((CHUNKS, ROWS, CHUNK), BF16),
-            pltpu.VMEM((2, ROWS, CHUNK), BF16),
+            pltpu.VMEM((ROWS, CHUNK), BF16),
             pltpu.VMEM((2, CHUNKS, HALF, CHUNK), BF16),
             pltpu.VMEM((CHUNKS, HALF, CHUNK), BF16),
             pltpu.VMEM((CHUNKS, HALF, CHUNK), BF16),
@@ -558,19 +595,19 @@
             pltpu.VMEM((2, HALF, CHUNK), BF16),
             pltpu.VMEM((ROWS, CHUNK), F32),
             pltpu.VMEM((NZ, ROWS, 2 * HEAD), F32),
-            pltpu.VMEM((3, 8, 8, 128), F32),
+            pltpu.VMEM((3, 8, 1, 128), F32),
             pltpu.SemaphoreType.DMA((6,)),
             pltpu.SemaphoreType.DMA((MAX_COPIES,)),
             pltpu.SemaphoreType.DMA((MAX_COPIES,)),
         ],
         compiler_params=pltpu.CompilerParams(
-            collective_id=0, has_side_effects=True, vmem_limit_bytes=48 * 1024 * 1024
+            collective_id=0, has_side_effects=True, vmem_limit_bytes=VMEM_LIMIT
         ),
     )(
         lengths,
         t_index,
-        latents,
-        mod_scale.reshape(CHUNKS, CHUNK),
+        latents.T,
+        mod_scale.reshape(1, WIDTH),
         q_weight,
         k_weight,
         v_weight,
@@ -579,7 +616,7 @@
         k_gain.reshape(1, HEAD),
         student_weight,
     )
-    return (target, student, loss.reshape(()))
+    return (target.T, student.T, loss.reshape(()))
 
 
 def solution(mesh):

time: 130 us -> 116 us (0.89)
  local copies, waits for them, and re-layouts: 11.5 us -> 2.84 us
  Pallas kernels: 116 us -> 109 us
    unnamed x21 -> x2, local copies, waits for them, and re-layouts: 10.8 us -> 2.84 us
    pallas_call x1, Pallas kernels: 116 us -> 109 us  [on_device(): pl.pallas_call(kernel, out_shape=(jax.ShapeDtypeStruct((192, ROWS), BF16)...]
where the time goes in v2:
time: 116 us; the launch traced here: 115 us
  Pallas kernels  109 us (94%)
  local copies, waits for them, and re-layouts  2.84 us (2%)
  between operations  2.46 us (2%)
    pallas_call x1, Pallas kernels, on_device(): pl.pallas_call(kernel, out_shape=(jax.ShapeDtypeStruct((192, ROWS), BF16)...  109 us
    unnamed x2, local copies, waits for them, and re-layouts  2.84 us

profile of v2, /device:TPU:1, one launch (start us, length us, event | category | flops | bytes accessed | tf_op | source)
XLA Modules:
  0.0 114.5 jit_solution(10560225407004328188)
XLA Ops:
  0.6 109.2 %shard_map.130 = (bf16[192,128]{1,0:T(8,128)(2,1)}, bf16[192,128]{1,0:T(8,128)(2,1)}, f32[1,1]{1,0:T(1,128)}) custom-call(s32[2]{0:T(128)} %lengths_ref.1, s32[2]{0:T(128)} %t_index_ref.1, bf16[192,128]{1,0:T(8,128)(2,1)} %bitcast.7, f32[1,3072]{1,0:T(1,128)} %bitcast.10, bf16[3072,128]{1,0:T(8,128)(2,1)} %wq_hbm.1, bf16[3072,128]{1,0:T(8,128)(2,1)} %wk_hbm.1, ...), custom_call_target="tpu_custom_call" | custom-call | tf_op jit(solution)/shard_map/pallas_call | solution.py:564
  109.9 1.4 %copy.17 = bf16[128,192]{0,1:T(8,128)(2,1)} copy(bf16[128,192]{0,1:T(8,128)(2,1)} %bitcast.9) | data formatting | bytes 98304
  111.3 1.4 %copy.18 = bf16[128,192]{0,1:T(8,128)(2,1)} copy(bf16[128,192]{0,1:T(8,128)(2,1)} %bitcast.8) | data formatting | bytes 98304

commit v3 on v2

--- a/solution.py
+++ b/solution.py
@@ -25,19 +25,18 @@
 
 
 def kernel(
-    lengths_ref,
-    t_index_ref,
+    lengths_hbm,
+    t_index_hbm,
     latents_hbm,
-    mod_ref,
+    mod_hbm,
     wq_hbm,
     wk_hbm,
     wv_hbm,
     wo_hbm,
-    q_gain_ref,
-    k_gain_ref,
+    q_gain_hbm,
+    k_gain_hbm,
     ws_hbm,
-    target_ref,
-    student_ref,
+    both_ref,
     loss_ref,
     xt,
     wqkv,
@@ -64,6 +63,11 @@
     acc_qkv,
     acc_o,
     lossbuf,
+    lengths_ref,
+    t_index_ref,
+    mod_ref,
+    q_gain_ref,
+    k_gain_ref,
     local_sem,
     send_sem,
     recv_sem,
@@ -82,8 +86,13 @@
         pltpu.make_async_copy(wv_hbm, wqkv.at[:, 2 * HEAD : 3 * HEAD], local_sem.at[3]),
         pltpu.make_async_copy(wo_hbm, wo, local_sem.at[4]),
         pltpu.make_async_copy(ws_hbm, ws, local_sem.at[5]),
+        pltpu.make_async_copy(lengths_hbm, lengths_ref, local_sem.at[6]),
+        pltpu.make_async_copy(t_index_hbm, t_index_ref, local_sem.at[7]),
+        pltpu.make_async_copy(mod_hbm, mod_ref, local_sem.at[8]),
+        pltpu.make_async_copy(q_gain_hbm, q_gain_ref, local_sem.at[9]),
+        pltpu.make_async_copy(k_gain_hbm, k_gain_ref, local_sem.at[10]),
     ]
-    for load in loads:
+    for load in loads[:1] + loads[6:]:
         load.start()
 
     barrier = pltpu.get_barrier_semaphore()
@@ -94,7 +103,8 @@
     peers += [{"tp_0": lax.rem(x + d, NX), "tp_2": other} for d in range(NX)]
     for peer in peers:
         pl.semaphore_signal(barrier, inc=1, device_id=peer, device_id_type=MESH)
-    loads[0].wait()
+    for load in loads[:1] + loads[6:]:
+        load.wait()
     pl.semaphore_wait(barrier, len(peers))
 
     count = [0]
@@ -142,28 +152,35 @@
 
     own_chunk = 2 * x + zh
 
-    def piece(chunk, which):
-        return xt.at[chunk, pl.ds(pl.multiple_of(which * 192, 192), 192), :]
-
-    k_z = slot()
-    send(piece(own_chunk, c), piece(own_chunk, c), k_z, tp_1=1 - zh)
-    k_x = [[slot() for _ in range(1, NX)] for _ in range(2)]
+    def piece(chunk, which, h=None):
+        start, size = (which * 192, 192) if h is None else (which * 192 + h * 96, 96)
+        return xt.at[chunk, pl.ds(pl.multiple_of(start, size), size), :]
+
+    k_z = [slot(), slot()]
+    k_x = [[[slot(), slot()] for _ in range(1, NX)] for _ in range(2)]
     k_c = [slot() for _ in range(CHUNKS)]
+    for h in range(2):
+        send(piece(own_chunk, c, h), piece(own_chunk, c, h), k_z[h], tp_1=1 - zh)
     for d in range(1, NX):
-        send(piece(own_chunk, c), piece(own_chunk, c), k_x[0][d - 1], tp_0=x_at(d))
+        send(piece(own_chunk, c), piece(own_chunk, c), k_x[0][d - 1][0], tp_0=x_at(d))
     send(piece(own_chunk, c), piece(own_chunk, c), k_c[0], tp_2=other)
+    for load in loads[1:4]:
+        load.start()
     arrivals = [own_chunk]
+    far_chunk = 2 * x + 1 - zh
+    for h in range(2):
+        arrived(piece(far_chunk, c, h), k_z[h], tp_1=1 - zh)
+        for d in range(1, NX):
+            send(piece(far_chunk, c, h), piece(far_chunk, c, h), k_x[1][d - 1][h], tp_0=x_at(d))
     for d in range(1, NX):
         chunk = 2 * x_at(-d) + zh
-        arrived(piece(chunk, c), k_x[0][d - 1], tp_0=x_at(-d))
+        arrived(piece(chunk, c), k_x[0][d - 1][0], tp_0=x_at(-d))
         send(piece(chunk, c), piece(chunk, c), k_c[d], tp_2=other)
         arrivals.append(chunk)
-    far_chunk = 2 * x + 1 - zh
-    arrived(piece(far_chunk, c), k_z, tp_1=1 - zh)
-    for d in range(1, NX):
-        send(piece(far_chunk, c), piece(far_chunk, c), k_x[1][d - 1], tp_0=x_at(d))
     send(piece(far_chunk, c), piece(far_chunk, c), k_c[NX], tp_2=other)
     arrivals.append(far_chunk)
+    for load in loads[4:6]:
+        load.start()
 
     for load in loads[1:4]:
         load.wait()
@@ -196,7 +213,8 @@
             own_hidden = hidden
     for d in range(1, NX):
         chunk = 2 * x_at(-d) + 1 - zh
-        arrived(piece(chunk, c), k_x[1][d - 1], tp_0=x_at(-d))
+        for h in range(2):
+            arrived(piece(chunk, c, h), k_x[1][d - 1][h], tp_0=x_at(-d))
         send(piece(chunk, c), piece(chunk, c), k_c[NX + d], tp_2=other)
         arrivals.append(chunk)
     for number in range(NX + 1, CHUNKS):
@@ -215,34 +233,44 @@
         qbuf[e, z] = head_norm(scaled[:, 0:HEAD], q_gain_ref[...])
         kvbuf[e, y, 0] = head_norm(scaled[:, HEAD : 2 * HEAD], k_gain_ref[...])
         kvbuf[e, y, 1] = scaled[:, 2 * HEAD : 3 * HEAD].astype(BF16)
-        up, down = lax.rem(y + 1, NY), lax.rem(y + NY - 1, NY)
         k_ring = [[[slot(), slot()] for _ in range(4)] for _ in range(2)]
         k_q = [slot() for _ in range(1, NZ)]
 
         def part(owner, which):
             return kvbuf.at[e, owner, which]
 
-        def pass_on(owner, which, direction, hop):
-            target = up if direction == 0 else down
-            send(part(owner, which), part(owner, which), k_ring[direction][hop][which], seq_1=target)
-
-        for which in range(2):
-            for direction in range(2):
-                pass_on(y, which, direction, 0)
+        def at(distance):
+            return lax.rem(y + distance + NY, NY)
+
+        def pass_on(owner, which, direction, distance, hops):
+            target = at(hops if direction == 0 else -hops)
+            send(
+                part(owner, which), part(owner, which), k_ring[direction][distance - 1][which], seq_1=target
+            )
+
+        for hops in (2, 1):
+            for which in range(2):
+                for direction in range(2):
+                    pass_on(y, which, direction, hops, hops)
         for d in range(1, NZ):
             send(qbuf.at[e, z], qbuf.at[e, z], k_q[d - 1], seq_0=lax.rem(z + d, NZ))
         while_waiting[0]()
 
-        def take(hop):
-            owners = (lax.rem(y + NY - hop, NY), lax.rem(y + hop, NY))
+        came_by = (1, 2, 1, 2)
+
+        def take(distance):
+            owners = (at(-distance), at(distance))
             for which in range(2):
                 for direction in range(2):
-                    if hop == 4 and which != direction:
+                    if distance == 4 and which != direction:
                         continue
-                    source = down if direction == 0 else up
-                    arrived(part(owners[direction], which), k_ring[direction][hop - 1][which], seq_1=source)
-                    if hop < 3 or (hop == 3 and which == direction):
-                        pass_on(owners[direction], which, direction, hop)
+                    hops = came_by[distance - 1]
+                    source = at(-hops if direction == 0 else hops)
+                    arrived(part(owners[direction], which), k_ring[direction][distance - 1][which], seq_1=source)
+                    if distance == 2:
+                        pass_on(owners[direction], which, direction, 3, 1)
+                        if which == direction:
+                            pass_on(owners[direction], which, direction, 4, 2)
             return owners
 
         queries_from = [lax.rem(z + d, NZ) for d in range(NZ)]
@@ -264,16 +292,15 @@
                 else:
                     acc_o[i] += term
 
-        around = take(1)
+        near = take(2) + take(1)
         for d in range(1, NZ):
             source = lax.rem(z + NZ - d, NZ)
             arrived(qbuf.at[e, source], k_q[d - 1], seq_0=source)
         block(y, True)
-        for owner in around:
+        for owner in near:
             block(owner, False)
-        for hop in (2, 3):
-            for owner in take(hop):
-                block(owner, False)
+        for owner in take(3):
+            block(owner, False)
         block(take(4)[0], False)
 
         k_e = [slot() for _ in range(1, NZ)]
@@ -424,7 +451,6 @@
     for h in range(2):
         arrived(vpart(2 * x + other, h), k_vc[h][0], tp_2=other)
     squares = state_chunk(1, 2 * x + other, squares)
-    student_core()
     for h in range(2):
         for d in range(1, NX):
             theirs = 2 * x_at(-d) + c
@@ -439,7 +465,7 @@
         squares = state_chunk(2 * d + 1, last, squares)
 
     inverse = lax.rsqrt(squares * (1.0 / WIDTH) + EPS)
-    attended = attention(1, inverse, (nothing, nothing))
+    attended = attention(1, inverse, (student_core, nothing))
 
     adds, helps = c == zh, c != zh
     k_v1 = [slot(), slot()]
@@ -457,6 +483,20 @@
             partner_copy(h).start()
 
     partial_velocity(1, attended, nothing, to_partner_if_needed)
+
+    arrived(ubuf.at[other], k_su, tp_2=other)
+    student_whole = jnp.concatenate([ubuf[0], ubuf[1]], axis=0).astype(F32)
+    start_whole = vbuf[own_chunk].astype(F32)
+    lanes = lane_iota
+    k_l = [[slot(), slot()] for _ in range(NX)]
+
+    def loss_row(d, flip):
+        row = lossbuf.at[0, x]
+        return remote(row, row, k_l[d][flip], tp_0=x_at(d), tp_2=c if flip == 0 else other)
+
+    def loss_row_from(d, flip):
+        row = lossbuf.at[0, x_at(-d)]
+        return remote(row, row, k_l[d][flip], tp_0=x_at(-d), tp_2=c if flip == 0 else other)
 
     @pl.when(adds)
     def _():
@@ -464,38 +504,45 @@
             partner_copy(h).wait_recv()
             v1buf[h * HALF : (h + 1) * HALF, :] = both_partials(1, h)
             sibling_copy(h).start()
-
-    arrived(ubuf.at[other], k_su, tp_2=other)
-    student = half_columns(jnp.concatenate([ubuf[0], ubuf[1]], axis=0).astype(F32))
-    student_ref[...] = student.T.astype(BF16)
-    start_velocity = half_columns(vbuf[own_chunk].astype(F32))
+        whole = (0.5 * (start_whole + v1buf[...].astype(F32))).astype(BF16).astype(F32)
+        residual = student_whole - whole
+        per_token = jnp.sum(
+            residual * residual + KINETIC * (student_whole * student_whole), axis=1, keepdims=True
+        )
+        first_sum = jnp.sum(jnp.where(in_first, per_token, 0.0), axis=0, keepdims=True)
+        second_sum = jnp.sum(jnp.where(in_first, 0.0, per_token), axis=0, keepdims=True)
+        lossbuf[0, x] = jnp.where(lanes == 0, first_sum, jnp.where(lanes == 1, second_sum, 0.0))
+        for d in range(NX):
+            for flip in range(2):
+                if d or flip:
+                    loss_row(d, flip).start()
+
+    both_ref[1] = half_columns(student_whole).T.astype(BF16)
 
     @pl.when(helps)
     def _():
         for h in range(2):
             sibling_copy(h).wait_recv()
             partner_copy(h).wait_send()
+        for d in range(NX):
+            loss_row_from(d, 1).wait_recv()
 
     @pl.when(adds)
     def _():
-        for h in range(2):
-            sibling_copy(h).wait_send()
-
-    end_velocity = half_columns(v1buf[...].astype(F32))
-    target = (0.5 * (start_velocity + end_velocity)).astype(BF16).astype(F32)
-    target_ref[...] = target.T.astype(BF16)
-    residual = student - target
-    per_token = jnp.sum(residual * residual + KINETIC * (student * student), axis=1, keepdims=True)
-    first_sum = jnp.sum(jnp.where(in_first, per_token, 0.0), axis=0, keepdims=True)
-    second_sum = jnp.sum(jnp.where(in_first, 0.0, per_token), axis=0, keepdims=True)
-    lanes = lane_iota
-    sums = jnp.where(lanes == 0, first_sum, jnp.where(lanes == 1, second_sum, 0.0))
+        for d in range(1, NX):
+            loss_row_from(d, 0).wait_recv()
+
+    sums = lossbuf[0, 0]
+    for i in range(1, NX):
+        sums = sums + lossbuf[0, i]
 
     def exchanged(stage, own, others, sums):
         lossbuf[stage, own] = sums
         numbers = [slot() for _ in others]
         for number, (where, target, source) in zip(numbers, others):
             send(lossbuf.at[stage, own], lossbuf.at[stage, own], number, **where(target))
+        if stage == 1:
+            both_ref[0] = half_columns(0.5 * (start_whole + v1buf[...].astype(F32))).T.astype(BF16)
         for number, (where, target, source) in zip(numbers, others):
             index = source[0]
             arrived(lossbuf.at[stage, index], number, **where(source))
@@ -504,24 +551,12 @@
             total = total + lossbuf[stage, i]
         return total
 
-    def over_x(place):
-        return {"tp_0": place[1], "tp_2": place[2]}
-
     def over_y(place):
         return {"seq_1": place[0]}
 
     def over_z(place):
         return {"tp_1": place[1], "seq_0": place[2]}
 
-    x_others = []
-    for d in range(NX):
-        for core in (c, other):
-            if d == 0 and core is c:
-                continue
-            x_others.append(
-                (over_x, (None, x_at(d), core), (2 * x_at(-d) + core, x_at(-d), core))
-            )
-    sums = exchanged(0, 2 * x + c, x_others, sums)
     y_others = [
         (over_y, (lax.rem(y + d, NY),), (lax.rem(y + NY - d, NY),)) for d in range(1, NY)
     ]
@@ -541,6 +576,15 @@
     )
     loss_ref[0, 0] = 0.5 * jnp.sum(sums * scale)
 
+    @pl.when(adds)
+    def _():
+        for h in range(2):
+            sibling_copy(h).wait_send()
+        for d in range(NX):
+            for flip in range(2):
+                if d or flip:
+                    loss_row(d, flip).wait_send()
+
     for copy in sends:
         copy.wait_send()
 
@@ -561,15 +605,14 @@
     smem = pl.BlockSpec(memory_space=pltpu.SMEM)
     vmem = pl.BlockSpec(memory_space=pltpu.VMEM)
     anywhere = pl.BlockSpec(memory_space=pl.ANY)
-    target, student, loss = pl.pallas_call(
+    both, loss = pl.pallas_call(
         kernel,
         out_shape=(
-            jax.ShapeDtypeStruct((192, ROWS), BF16),
-            jax.ShapeDtypeStruct((192, ROWS), BF16),
+            jax.ShapeDtypeStruct((2, 192, ROWS), BF16),
             jax.ShapeDtypeStruct((1, 1), F32),
         ),
-        in_specs=[smem, smem, anywhere, vmem, anywhere, anywhere, anywhere, anywhere, vmem, vmem, anywhere],
-        out_specs=(vmem, vmem, smem),
+        in_specs=[anywhere] * 11,
+        out_specs=(vmem, smem),
         scratch_shapes=[
             pltpu.VMEM((CHUNKS, CHUNK, ROWS), BF16),
             pltpu.VMEM((WIDTH, CHUNK), BF16),
@@ -596,7 +639,12 @@
             pltpu.VMEM((ROWS, CHUNK), F32),
             pltpu.VMEM((NZ, ROWS, 2 * HEAD), F32),
             pltpu.VMEM((3, 8, 1, 128), F32),
-            pltpu.SemaphoreType.DMA((6,)),
+            pltpu.SMEM((2,), jnp.int32),
+            pltpu.SMEM((2,), jnp.int32),
+            pltpu.VMEM((1, WIDTH), F32),
+            pltpu.VMEM((1, HEAD), F32),
+            pltpu.VMEM((1, HEAD), F32),
+            pltpu.SemaphoreType.DMA((11,)),
             pltpu.SemaphoreType.DMA((MAX_COPIES,)),
             pltpu.SemaphoreType.DMA((MAX_COPIES,)),
         ],
@@ -616,7 +664,7 @@
         k_gain.reshape(1, HEAD),
         student_weight,
     )
-    return (target.T, student.T, loss.reshape(()))
+    return (both[0].T, both[1].T, loss.reshape(()))
 
 
 def solution(mesh):

time: 116 us -> 108 us (0.931)
  Pallas kernels: 109 us -> 104 us
  local copies, waits for them, and re-layouts: 2.84 us -> 1.47 us
    pallas_call x1, Pallas kernels: 109 us -> 104 us  [on_device(): pl.pallas_call(kernel, out_shape=(jax.ShapeDtypeStruct((2, 192, ROWS), BF...]
    unnamed x2 -> x0, local copies, waits for them, and re-layouts: 2.84 us -> none
    transpose x0 -> x1, local copies, waits for them, and re-layouts: none -> 1.47 us  [on_device(): return (both[0].T, both[1].T, loss.reshape(()))]
where the time goes in v3:
time: 108 us; the launch traced here: 107 us
  Pallas kernels  104 us (96%)
  between operations  2.33 us (2%)
  local copies, waits for them, and re-layouts  1.47 us (1%)
    pallas_call x1, Pallas kernels, on_device(): pl.pallas_call(kernel, out_shape=(jax.ShapeDtypeStruct((2, 192, ROWS), BF...  104 us

profile of v3, /device:TPU:1, one launch (start us, length us, event | category | flops | bytes accessed | tf_op | source)
XLA Modules:
  0.0 107.4 jit_solution(4166743876989367320)
XLA Ops:
  0.6 103.6 %shard_map.130 = (bf16[2,192,128]{2,1,0:T(8,128)(2,1)}, f32[1,1]{1,0:T(1,128)}) custom-call(s32[2]{0:T(128)} %lengths_hbm.1, s32[2]{0:T(128)} %t_index_hbm.1, bf16[192,128]{1,0:T(8,128)(2,1)} %bitcast.13, f32[1,3072]{1,0:T(1,128)} %bitcast.14, bf16[3072,128]{1,0:T(8,128)(2,1)} %wq_hbm.1, bf16[3072,128]{1,0:T(8,128)(2,1)} %wk_hbm.1, ...), custom_call_target="tpu_custom_call" | custom-call | tf_op jit(solution)/shard_map/pallas_call | solution.py:608
  104.2 1.5 %slice_bitcast_fusion = (bf16[128,192]{0,1:T(8,128)(2,1)}, bf16[128,192]{0,1:T(8,128)(2,1)}) fusion(bf16[2,192,128]{2,1,0:T(8,128)(2,1)} %get-tuple-element.5), kind=kLoop, calls=%fused_computation | loop fusion | bytes 196608 | tf_op jit(solution)/shard_map/transpose | solution.py:667

commit v4 on v3

--- a/solution.py
+++ b/solution.py
@@ -20,7 +20,10 @@
 KINETIC = 0.1
 STEP = 0.125
 EXP_SCALE = math.log2(math.e) / math.sqrt(HEAD)
-MAX_COPIES = 224
+MAX_COPIES = 250
+PARTS = 4
+FAR_FIRST = (2, 1, 3)
+PART = ROWS // PARTS
 VMEM_LIMIT = 67043328
 
 
@@ -36,7 +39,7 @@
     q_gain_hbm,
     k_gain_hbm,
     ws_hbm,
-    both_ref,
+    both_hbm,
     loss_ref,
     xt,
     wqkv,
@@ -63,6 +66,7 @@
     acc_qkv,
     acc_o,
     lossbuf,
+    both_ref,
     lengths_ref,
     t_index_ref,
     mod_ref,
@@ -161,7 +165,7 @@
     k_c = [slot() for _ in range(CHUNKS)]
     for h in range(2):
         send(piece(own_chunk, c, h), piece(own_chunk, c, h), k_z[h], tp_1=1 - zh)
-    for d in range(1, NX):
+    for d in FAR_FIRST:
         send(piece(own_chunk, c), piece(own_chunk, c), k_x[0][d - 1][0], tp_0=x_at(d))
     send(piece(own_chunk, c), piece(own_chunk, c), k_c[0], tp_2=other)
     for load in loads[1:4]:
@@ -170,7 +174,7 @@
     far_chunk = 2 * x + 1 - zh
     for h in range(2):
         arrived(piece(far_chunk, c, h), k_z[h], tp_1=1 - zh)
-        for d in range(1, NX):
+        for d in FAR_FIRST:
             send(piece(far_chunk, c, h), piece(far_chunk, c, h), k_x[1][d - 1][h], tp_0=x_at(d))
     for d in range(1, NX):
         chunk = 2 * x_at(-d) + zh
@@ -268,9 +272,9 @@
                     source = at(-hops if direction == 0 else hops)
                     arrived(part(owners[direction], which), k_ring[direction][distance - 1][which], seq_1=source)
                     if distance == 2:
-                        pass_on(owners[direction], which, direction, 3, 1)
                         if which == direction:
                             pass_on(owners[direction], which, direction, 4, 2)
+                        pass_on(owners[direction], which, direction, 3, 1)
             return owners
 
         queries_from = [lax.rem(z + d, NZ) for d in range(NZ)]
@@ -330,33 +334,23 @@
 
     def partial_velocity(e, attended, while_waiting, hand_on):
         own = 2 * x + c
-        k_a = [[[slot(), slot()] for _ in range(NX)] for _ in range(2)]
-        for h in range(2):
-            abuf[e, h, own] = attended[h * HALF : (h + 1) * HALF]
-            for d in range(NX):
-                for flip in range(2):
-                    if d == 0 and flip == 0:
-                        continue
-                    send(
-                        abuf.at[e, h, own],
-                        abuf.at[e, h, own],
-                        k_a[h][d][flip],
-                        tp_0=x_at(d),
-                        tp_2=c if flip == 0 else other,
-                    )
+        k_a = [[slot(), slot()] for _ in range(NX)]
+        abuf[e, own] = attended
+        for d in FAR_FIRST:
+            send(abuf.at[e, own], abuf.at[e, own], k_a[d][0], tp_0=x_at(d))
+        send(abuf.at[e, own], abuf.at[e, own], k_a[0][1], tp_2=other)
         while_waiting()
-        for h in range(2):
-            for d in range(NX):
-                for flip in range(2):
-                    if d == 0 and flip == 0:
-                        continue
-                    core = c if flip == 0 else other
-                    arrived(
-                        abuf.at[e, h, 2 * x_at(-d) + core], k_a[h][d][flip], tp_0=x_at(-d), tp_2=core
-                    )
-            heads = jnp.concatenate([abuf[e, h, i] for i in range(CHUNKS)], axis=1)
-            partial = jnp.dot(heads, wcols[...].reshape(INNER, CHUNK), preferred_element_type=F32)
-            pbuf[e, 0, h] = partial.astype(BF16)
+        for d in range(1, NX):
+            part = abuf.at[e, 2 * x_at(-d) + c]
+            arrived(part, k_a[d][0], tp_0=x_at(-d))
+            send(part, part, k_a[d][1], tp_2=other)
+        for d in range(NX):
+            arrived(abuf.at[e, 2 * x_at(-d) + other], k_a[d][1], tp_2=other)
+        heads = jnp.concatenate([abuf[e, i] for i in range(CHUNKS)], axis=1)
+        weights = wcols[...].reshape(INNER, CHUNK)
+        for h in range(PARTS):
+            rows = heads[h * PART : (h + 1) * PART]
+            pbuf[e, 0, h] = jnp.dot(rows, weights, preferred_element_type=F32).astype(BF16)
             hand_on(h)
 
     def both_partials(e, h):
@@ -419,7 +413,7 @@
         pass
 
     attended = attention(0, inverse, (send_columns, student_x))
-    k_p = [[slot(), slot()] for _ in range(2)]
+    k_p = [[slot() for _ in range(PARTS)] for _ in range(2)]
 
     def to_partner(h):
         send(pbuf.at[0, 0, h], pbuf.at[0, 1, h], k_p[0][h], tp_1=1 - zh)
@@ -428,16 +422,16 @@
     student_z()
 
     own_slot = 2 * x + c
-    k_vx = [[slot() for _ in range(1, NX)] for _ in range(2)]
-    k_vc = [[slot() for _ in range(NX)] for _ in range(2)]
+    k_vx = [[slot() for _ in range(1, NX)] for _ in range(PARTS)]
+    k_vc = [[slot() for _ in range(NX)] for _ in range(PARTS)]
 
     def vpart(chunk, h):
-        return vbuf.at[chunk, h * HALF : (h + 1) * HALF, :]
-
-    for h in range(2):
+        return vbuf.at[chunk, h * PART : (h + 1) * PART, :]
+
+    for h in range(PARTS):
         arrived(pbuf.at[0, 1, h], k_p[0][h], tp_1=1 - zh)
-        vbuf[own_slot, h * HALF : (h + 1) * HALF, :] = both_partials(0, h)
-        for d in range(1, NX):
+        vbuf[own_slot, h * PART : (h + 1) * PART, :] = both_partials(0, h)
+        for d in FAR_FIRST:
             send(vpart(own_slot, h), vpart(own_slot, h), k_vx[h][d - 1], tp_0=x_at(d))
         send(vpart(own_slot, h), vpart(own_slot, h), k_vc[h][0], tp_2=other)
     squares = jnp.zeros((ROWS, 1), F32)
@@ -448,10 +442,10 @@
         return project_chunk(number, chunk, state.astype(F32), times, squares)[0]
 
     squares = state_chunk(0, own_slot, squares)
-    for h in range(2):
+    for h in range(PARTS):
         arrived(vpart(2 * x + other, h), k_vc[h][0], tp_2=other)
     squares = state_chunk(1, 2 * x + other, squares)
-    for h in range(2):
+    for h in range(PARTS):
         for d in range(1, NX):
             theirs = 2 * x_at(-d) + c
             arrived(vpart(theirs, h), k_vx[h][d - 1], tp_0=x_at(-d))
@@ -460,7 +454,7 @@
         squares = state_chunk(2 * d, 2 * x_at(-d) + c, squares)
     for d in range(1, NX):
         last = 2 * x_at(-d) + other
-        for h in range(2):
+        for h in range(PARTS):
             arrived(vpart(last, h), k_vc[h][d], tp_2=other)
         squares = state_chunk(2 * d + 1, last, squares)
 
@@ -468,13 +462,13 @@
     attended = attention(1, inverse, (student_core, nothing))
 
     adds, helps = c == zh, c != zh
-    k_v1 = [slot(), slot()]
+    k_v1 = [slot() for _ in range(PARTS)]
 
     def partner_copy(h):
         return remote(pbuf.at[1, 0, h], pbuf.at[1, 1, h], k_p[1][h], tp_1=1 - zh)
 
     def sibling_copy(h):
-        part = v1buf.at[h * HALF : (h + 1) * HALF, :]
+        part = v1buf.at[h * PART : (h + 1) * PART, :]
         return remote(part, part, k_v1[h], tp_2=other)
 
     def to_partner_if_needed(h):
@@ -500,9 +494,9 @@
 
     @pl.when(adds)
     def _():
-        for h in range(2):
+        for h in range(PARTS):
             partner_copy(h).wait_recv()
-            v1buf[h * HALF : (h + 1) * HALF, :] = both_partials(1, h)
+            v1buf[h * PART : (h + 1) * PART, :] = both_partials(1, h)
             sibling_copy(h).start()
         whole = (0.5 * (start_whole + v1buf[...].astype(F32))).astype(BF16).astype(F32)
         residual = student_whole - whole
@@ -521,7 +515,7 @@
 
     @pl.when(helps)
     def _():
-        for h in range(2):
+        for h in range(PARTS):
             sibling_copy(h).wait_recv()
             partner_copy(h).wait_send()
         for d in range(NX):
@@ -535,6 +529,8 @@
     sums = lossbuf[0, 0]
     for i in range(1, NX):
         sums = sums + lossbuf[0, i]
+
+    out_copy = pltpu.make_async_copy(both_ref, both_hbm, local_sem.at[11])
 
     def exchanged(stage, own, others, sums):
         lossbuf[stage, own] = sums
@@ -543,6 +539,7 @@
             send(lossbuf.at[stage, own], lossbuf.at[stage, own], number, **where(target))
         if stage == 1:
             both_ref[0] = half_columns(0.5 * (start_whole + v1buf[...].astype(F32))).T.astype(BF16)
+            out_copy.start()
         for number, (where, target, source) in zip(numbers, others):
             index = source[0]
             arrived(lossbuf.at[stage, index], number, **where(source))
@@ -578,13 +575,14 @@
 
     @pl.when(adds)
     def _():
-        for h in range(2):
+        for h in range(PARTS):
             sibling_copy(h).wait_send()
         for d in range(NX):
             for flip in range(2):
                 if d or flip:
                     loss_row(d, flip).wait_send()
 
+    out_copy.wait()
     for copy in sends:
         copy.wait_send()
 
@@ -603,7 +601,6 @@
     student_weight,
 ):
     smem = pl.BlockSpec(memory_space=pltpu.SMEM)
-    vmem = pl.BlockSpec(memory_space=pltpu.VMEM)
     anywhere = pl.BlockSpec(memory_space=pl.ANY)
     both, loss = pl.pallas_call(
         kernel,
@@ -612,7 +609,7 @@
             jax.ShapeDtypeStruct((1, 1), F32),
         ),
         in_specs=[anywhere] * 11,
-        out_specs=(vmem, smem),
+        out_specs=(anywhere, smem),
         scratch_shapes=[
             pltpu.VMEM((CHUNKS, CHUNK, ROWS), BF16),
             pltpu.VMEM((WIDTH, CHUNK), BF16),
@@ -625,8 +622,8 @@
             pltpu.VMEM((8, 128), F32),
             pltpu.VMEM((2, NZ, ROWS + 16, HEAD), BF16),
             pltpu.VMEM((2, NZ - 1, ROWS + 16, HEAD), BF16),
-            pltpu.VMEM((2, 2, CHUNKS, HALF, HEAD), BF16),
-            pltpu.VMEM((2, 2, 2, HALF, CHUNK), BF16),
+            pltpu.VMEM((2, CHUNKS, ROWS, HEAD), BF16),
+            pltpu.VMEM((2, 2, PARTS, PART, CHUNK), BF16),
             pltpu.VMEM((CHUNKS, ROWS, CHUNK), BF16),
             pltpu.VMEM((ROWS, CHUNK), BF16),
             pltpu.VMEM((2, CHUNKS, HALF, CHUNK), BF16),
@@ -639,12 +636,13 @@
             pltpu.VMEM((ROWS, CHUNK), F32),
             pltpu.VMEM((NZ, ROWS, 2 * HEAD), F32),
             pltpu.VMEM((3, 8, 1, 128), F32),
+            pltpu.VMEM((2, 192, ROWS), BF16),
             pltpu.SMEM((2,), jnp.int32),
             pltpu.SMEM((2,), jnp.int32),
             pltpu.VMEM((1, WIDTH), F32),
             pltpu.VMEM((1, HEAD), F32),
             pltpu.VMEM((1, HEAD), F32),
-            pltpu.SemaphoreType.DMA((11,)),
+            pltpu.SemaphoreType.DMA((12,)),
             pltpu.SemaphoreType.DMA((MAX_COPIES,)),
             pltpu.SemaphoreType.DMA((MAX_COPIES,)),
         ],

time: 108 us -> 107 us (level)
  Pallas kernels: 104 us -> 102 us
    pallas_call x1, Pallas kernels: 104 us -> 102 us  [on_device(): pl.pallas_call(kernel, out_shape=(jax.ShapeDtypeStruct((2, 192, ROWS), BF...]
where the time goes in v4:
time: 107 us; the launch traced here: 106 us
  Pallas kernels  102 us (95%)
  between operations  2.33 us (2%)
  local copies, waits for them, and re-layouts  1.47 us (1%)
    pallas_call x1, Pallas kernels, on_device(): pl.pallas_call(kernel, out_shape=(jax.ShapeDtypeStruct((2, 192, ROWS), BF...  102 us

profile of v4, /device:TPU:1, one launch (start us, length us, event | category | flops | bytes accessed | tf_op | source)
XLA Modules:
  0.0 105.8 jit_solution(4216853493936720123)
XLA Ops:
  0.6 102.0 %shard_map.130 = (bf16[2,192,128]{2,1,0:T(8,128)(2,1)}, f32[1,1]{1,0:T(1,128)}) custom-call(s32[2]{0:T(128)} %lengths_hbm.1, s32[2]{0:T(128)} %t_index_hbm.1, bf16[192,128]{1,0:T(8,128)(2,1)} %bitcast.13, f32[1,3072]{1,0:T(1,128)} %bitcast.14, bf16[3072,128]{1,0:T(8,128)(2,1)} %wq_hbm.1, bf16[3072,128]{1,0:T(8,128)(2,1)} %wk_hbm.1, ...), custom_call_target="tpu_custom_call" | custom-call | tf_op jit(solution)/shard_map/pallas_call | solution.py:605
  102.7 1.5 %slice_bitcast_fusion = (bf16[128,192]{0,1:T(8,128)(2,1)}, bf16[128,192]{0,1:T(8,128)(2,1)}) fusion(bf16[2,192,128]{2,1,0:T(8,128)(2,1)} %get-tuple-element.5), kind=kLoop, calls=%fused_computation | loop fusion | bytes 196608 | tf_op jit(solution)/shard_map/transpose | solution.py:665

commit v5 on v4

--- a/solution.py
+++ b/solution.py
@@ -348,9 +348,9 @@
             arrived(abuf.at[e, 2 * x_at(-d) + other], k_a[d][1], tp_2=other)
         heads = jnp.concatenate([abuf[e, i] for i in range(CHUNKS)], axis=1)
         weights = wcols[...].reshape(INNER, CHUNK)
+        partial = jnp.dot(heads, weights, preferred_element_type=F32).astype(BF16)
         for h in range(PARTS):
-            rows = heads[h * PART : (h + 1) * PART]
-            pbuf[e, 0, h] = jnp.dot(rows, weights, preferred_element_type=F32).astype(BF16)
+            pbuf[e, 0, h] = partial[h * PART : (h + 1) * PART]
             hand_on(h)
 
     def both_partials(e, h):

time: 107 us -> 107 us (level)
  no operation moved by 1% of the time
where the time goes in v5:
time: 107 us; the launch traced here: 106 us
  Pallas kernels  102 us (95%)
  between operations  2.33 us (2%)
  local copies, waits for them, and re-layouts  1.47 us (1%)
    pallas_call x1, Pallas kernels, on_device(): pl.pallas_call(kernel, out_shape=(jax.ShapeDtypeStruct((2, 192, ROWS), BF...  102 us

profile of v5, /device:TPU:1, one launch (start us, length us, event | category | flops | bytes accessed | tf_op | source)
XLA Modules:
  0.0 105.9 jit_solution(11690108443008213459)
XLA Ops:
  0.6 102.1 %shard_map.130 = (bf16[2,192,128]{2,1,0:T(8,128)(2,1)}, f32[1,1]{1,0:T(1,128)}) custom-call(s32[2]{0:T(128)} %lengths_hbm.1, s32[2]{0:T(128)} %t_index_hbm.1, bf16[192,128]{1,0:T(8,128)(2,1)} %bitcast.13, f32[1,3072]{1,0:T(1,128)} %bitcast.14, bf16[3072,128]{1,0:T(8,128)(2,1)} %wq_hbm.1, bf16[3072,128]{1,0:T(8,128)(2,1)} %wk_hbm.1, ...), custom_call_target="tpu_custom_call" | custom-call | tf_op jit(solution)/shard_map/pallas_call | solution.py:605
  102.7 1.5 %slice_bitcast_fusion = (bf16[128,192]{0,1:T(8,128)(2,1)}, bf16[128,192]{0,1:T(8,128)(2,1)}) fusion(bf16[2,192,128]{2,1,0:T(8,128)(2,1)} %get-tuple-element.5), kind=kLoop, calls=%fused_computation | loop fusion | bytes 196608 | tf_op jit(solution)/shard_map/transpose | solution.py:665
